TPU v7x, 32 devices: a whole 2x2x4 slice. The times are simulated.
32 devices in a mesh: dp: 8 (over z, x), tensor: 4 (over y, core).
Axes of the slice: x: 2, y: 2, z: 4, core: 2. Of those that a mesh axis runs over, the one named last changes fastest.
Arguments:
- block_input: bfloat16 [8192, 1536], P(('dp', 'tensor')), may hold values from -6 to 6
- gain_attention: float32 [1536], replicated, may hold values from 0.1 to 1.9
- gain_feedforward: float32 [1536], replicated, may hold values from 0.1 to 1.9
- w_query: bfloat16 [1536, 1536], P(None, 'tensor'), as said below
- w_key: bfloat16 [1536, 768], P(None, 'tensor'), as said below
- w_value: bfloat16 [1536, 768], P(None, 'tensor'), may hold values from -0.15625 to 0.15625
- w_output: bfloat16 [1536, 1536], P('tensor'), may hold values from -1.25 to 1.25
- w_gate: bfloat16 [1536, 4096], P(None, 'tensor'), may hold values from -0.15625 to 0.15625
- w_up: bfloat16 [1536, 4096], P(None, 'tensor'), may hold values from -0.15625 to 0.15625
- w_down: bfloat16 [4096, 1536], P('tensor'), may hold values from -0.09375 to 0.09375
- cotangent: bfloat16 [8192, 1536], P(('dp', 'tensor')), may hold values from -12 to 12
Outputs:
- block_output: bfloat16 [8192, 1536], P(('dp', 'tensor'))
- input_grad: bfloat16 [8192, 1536], P(('dp', 'tensor'))
- grad_gain_attention: float32 [1536], replicated
- grad_gain_feedforward: float32 [1536], replicated
- grad_query: float32 [1536, 1536], P(None, 'tensor')
- grad_key: float32 [1536, 768], P(None, 'tensor')
- grad_value: float32 [1536, 768], P(None, 'tensor')
- grad_output: float32 [1536, 1536], P('tensor')
- grad_gate: float32 [1536, 4096], P(None, 'tensor')
- grad_up: float32 [1536, 4096], P(None, 'tensor')
- grad_down: float32 [4096, 1536], P('tensor')
Inputs may be any that keep to these rules, and one draw needn't show every extreme that they name: `w_query`: query projection. `w_key`: key projection with entries of order 1536^-0.5.
All inputs are finite; a program needn't handle non-finite values.
Results may differ from a plain program's by a relative error of at most 0.02.
Values may be sent and summed in bfloat16 or wider, within the bound.
No kernel may reach another device: no remote copies, remote signals or barrier semaphores. Data moves between devices by JAX's collectives and lax.ppermute only.
A program may use at most 192 MiB of HBM per device.

v0:
```python
import functools

import jax
import jax.numpy as jnp
from jax import lax
from jax.experimental import pallas as pl
from jax.experimental.pallas import tpu as pltpu
from jax.sharding import PartitionSpec as P


HD = 96
L = 1024
LANES = 128

EPS = 1e-05
THETA = 100000.0


def rope_tables(rows):
    half = HD // 2
    position = (jnp.arange(rows, dtype=jnp.int32) % L).astype(jnp.float32)[:, None]
    inverse = THETA ** (-jnp.arange(0, HD, 2, dtype=jnp.float32) / HD)
    angles = position * inverse[None, :]
    pad = ((0, 0), (0, LANES // 2 - half))
    cosine, sine = jnp.pad(jnp.cos(angles), pad), jnp.pad(jnp.sin(angles), pad)
    return (
        jnp.concatenate([cosine, cosine], axis=1),
        jnp.concatenate([-sine, sine], axis=1),
    )


def pad_halves(weight):
    split = weight.reshape(weight.shape[0], -1, 2, HD // 2)
    split = jnp.pad(split, ((0, 0), (0, 0), (0, 0), (0, LANES // 2 - HD // 2)))
    return split.reshape(weight.shape[0], -1)


def pad_heads(weight):
    split = weight.reshape(weight.shape[0], -1, HD)
    return jnp.pad(split, ((0, 0), (0, 0), (0, LANES - HD))).reshape(weight.shape[0], -1)


def pad_head_rows(weight):
    split = weight.reshape(-1, HD, weight.shape[1])
    return jnp.pad(split, ((0, 0), (0, LANES - HD), (0, 0))).reshape(-1, weight.shape[1])


def selection(columns, head, halves):
    lane = lax.broadcasted_iota(jnp.int32, (LANES, columns), 0)
    column = lax.broadcasted_iota(jnp.int32, (LANES, columns), 1)
    if halves:
        wide, half = LANES // 2, HD // 2
        upper = lane >= wide
        inner = jnp.where(upper, lane - wide, lane)
        target = jnp.where(inner < half, inner + jnp.where(upper, half, 0), -columns - LANES * 64)
    else:
        target = jnp.where(lane < HD, lane, -columns - LANES * 64)
    return jnp.where(target + head * HD == column, 1.0, 0.0).astype(jnp.bfloat16)


def dot(left, right, dims):
    return lax.dot_general(left, right, (dims, ((), ())), preferred_element_type=jnp.float32)


NN, NT, TN = ((1,), (0,)), ((1,), (1,)), ((0,), (0,))


def whole(shape):
    return pl.BlockSpec(shape, lambda *_: (0,) * len(shape), pipeline_mode=pl.Buffered(1))


def params(mebibytes, grid=True):
    return pltpu.CompilerParams(
        dimension_semantics=("arbitrary",) if grid else None,
        vmem_limit_bytes=mebibytes * 1024 * 1024,
    )


def cost(flops, moved, exps=0):
    return pl.CostEstimate(flops=int(flops), bytes_accessed=int(moved), transcendentals=int(exps))


def softmax_block(query, keys, block, step, span):
    scores = dot(query, keys, NT) * HD ** (-0.5)
    row = lax.broadcasted_iota(jnp.int32, scores.shape, 0)
    row = jnp.where(row >= step, row - step, row) + block * step
    column = lax.broadcasted_iota(jnp.int32, scores.shape, 1) + span
    scores = jnp.where(row >= column, scores, -jnp.inf)
    exponent = jnp.exp(scores - jnp.max(scores, axis=1, keepdims=True))
    return exponent * (1.0 / jnp.sum(exponent, axis=1, keepdims=True))


def turn(value, cosine, sine):
    return value * cosine + pltpu.roll(value, LANES // 2, 1) * sine


def unturn(value, cosine, sine):
    return value * cosine + pltpu.roll(value * sine, LANES // 2, 1)


def attend_kernel(pairs, step, qkv, cosine, sine, heads_out, flat_out, q_out, k_out, v_out):
    rows = cosine.shape[0]
    cos, sin = cosine[...], sine[...]
    for h in range(2 * pairs):
        q_out[:, h * LANES : (h + 1) * LANES] = turn(
            qkv[:, h * LANES : (h + 1) * LANES], cos, sin
        ).astype(jnp.bfloat16)
    for g in range(pairs):
        at = (2 * pairs + g) * LANES
        k_out[:, g * LANES : (g + 1) * LANES] = turn(
            qkv[:, at : at + LANES], cos, sin
        ).astype(jnp.bfloat16)
    at = 3 * pairs * LANES
    v_out[...] = qkv[:, at : at + pairs * LANES].astype(jnp.bfloat16)
    for g in range(pairs):
        kv = slice(g * LANES, (g + 1) * LANES)
        for block in range(rows // step):
            here = slice(block * step, (block + 1) * step)
            start = (block * step) // L * L
            past = slice(start, (block + 1) * step)
            one, two = (slice((2 * g + e) * LANES, (2 * g + e + 1) * LANES) for e in range(2))
            query = jnp.concatenate([q_out[here, one], q_out[here, two]], axis=0)
            prob = softmax_block(query, k_out[past, kv], block, step, start).astype(jnp.bfloat16)
            result = dot(prob, v_out[past, kv], NN).astype(jnp.bfloat16)
            heads_out[here, one] = result[:step]
            heads_out[here, two] = result[step:]
    flat = sum(
        dot(heads_out[:, h * LANES : (h + 1) * LANES], selection(2 * pairs * HD, h, False), NN)
        for h in range(2 * pairs)
    )
    flat_out[...] = flat.astype(jnp.bfloat16)


def attend(qkv, cosine, sine, pairs, step):
    rows = qkv.shape[0]
    shapes = [2 * pairs * LANES, 2 * pairs * HD, 2 * pairs * LANES, pairs * LANES, pairs * LANES]
    area = rows * min(rows, L) * 2 * pairs * 5 // 8
    return pl.pallas_call(
        functools.partial(attend_kernel, pairs, step),
        out_shape=[jax.ShapeDtypeStruct((rows, c), jnp.bfloat16) for c in shapes],
        compiler_params=params(26, False),
        cost_estimate=cost(4 * area * LANES, 10 * qkv.size, area),
        name="attend",
    )(qkv, cosine, sine)


def attend_back_kernel(pairs, step, group, *refs):
    q, k, v, heads, dheads, cosine, sine = refs[:7]
    out, dk, dv, dq = refs[-4:]
    rows = cosine.shape[0]
    cos, sin = cosine[...], sine[...]
    scale = HD ** (-0.5)
    width = 2 * pairs * HD
    flat_q = jnp.zeros((rows, width), jnp.float32)
    flat_kv = jnp.zeros((rows, width), jnp.float32)
    if len(refs) > 11:
        flat_q += refs[7][:, :width].astype(jnp.float32)
        flat_kv += refs[7][:, width:].astype(jnp.float32)
    for g in (group,):
        kv = slice(g * LANES, (g + 1) * LANES)
        dk[...] = jnp.zeros_like(dk)
        dv[...] = jnp.zeros_like(dv)
        for block in range(rows // step):
            here = slice(block * step, (block + 1) * step)
            start = (block * step) // L * L
            past = slice(start, (block + 1) * step)
            one, two = (slice((2 * g + e) * LANES, (2 * g + e + 1) * LANES) for e in range(2))

            def both(ref):
                return jnp.concatenate([ref[here, one], ref[here, two]], axis=0)

            query, dhead = both(q), both(dheads)
            prob = softmax_block(query, k[past, kv], block, step, start)
            dv[past] += dot(prob.astype(jnp.bfloat16), dhead, TN)
            delta = jnp.sum(
                dhead.astype(jnp.float32) * both(heads).astype(jnp.float32), axis=1, keepdims=True
            )
            dscore = (prob * (dot(dhead, v[past, kv], NT) - delta)).astype(jnp.bfloat16)
            dk[past] += dot(dscore, query, TN)
            dquery = dot(dscore, k[past, kv], NN)
            dq[0, here] = dquery[:step]
            dq[1, here] = dquery[step:]
        for e in range(2):
            back = unturn(dq[e] * scale, cos, sin).astype(jnp.bfloat16)
            flat_q += dot(back, selection(width, 2 * g + e, True), NN)
        back = unturn(dk[...] * scale, cos, sin).astype(jnp.bfloat16)
        flat_kv += dot(back, selection(width, g, True), NN)
        flat_kv += dot(dv[...].astype(jnp.bfloat16), selection(width, pairs + g, False), NN)
    out[:, :width] = flat_q.astype(jnp.bfloat16)
    out[:, width:] = flat_kv.astype(jnp.bfloat16)


def attend_back(q, k, v, heads, dheads, cosine, sine, pairs, step, group, before):
    rows = q.shape[0]
    area = rows * min(rows, L) * 2 * 5 // 8
    held = [] if before is None else [before]
    return pl.pallas_call(
        functools.partial(attend_back_kernel, pairs, step, group),
        out_shape=jax.ShapeDtypeStruct((rows, 4 * pairs * HD), jnp.bfloat16),
        scratch_shapes=[
            pltpu.VMEM((rows, LANES), jnp.float32),
            pltpu.VMEM((rows, LANES), jnp.float32),
            pltpu.VMEM((2, rows, LANES), jnp.float32),
        ],
        compiler_params=params(26, False),
        cost_estimate=cost(10 * area * LANES, 10 * q.size, area),
        name="attend_back",
    )(q, k, v, heads, dheads, cosine, sine, *held)


def place_kernel(count, me, *refs):
    for k in range(count):

        @pl.when(pl.program_id(0) == k)
        def _(k=k):
            refs[count][...] = refs[k][...]


def place(blocks, me):
    rows, columns = blocks[0].shape
    count = len(blocks)
    return pl.pallas_call(
        functools.partial(place_kernel, count),
        out_shape=jax.ShapeDtypeStruct((count * rows, columns), blocks[0].dtype),
        grid_spec=pltpu.PrefetchScalarGridSpec(
            num_scalar_prefetch=1,
            grid=(count,),
            in_specs=[whole((rows, columns))] * count,
            out_specs=pl.BlockSpec((rows, columns), lambda s, m: (m[0] ^ s, 0)),
        ),
        compiler_params=params(12),
        cost_estimate=cost(0, 4 * count * rows * columns),
        name="place",
    )(me, *blocks)


def norm_place_kernel(count, me, gain, *refs):
    for k in range(count):

        @pl.when(pl.program_id(0) == k)
        def _(k=k):
            refs[count + 1][...] = refs[k][...]
            value = refs[k][...].astype(jnp.float32)
            recip = lax.rsqrt(jnp.mean(value * value, axis=-1, keepdims=True) + EPS)
            refs[count][...] = (value * recip * gain[...]).astype(jnp.bfloat16)


def norm_place(blocks, gain, me):
    rows, columns = blocks[0].shape
    count = len(blocks)
    spot = pl.BlockSpec((rows, columns), lambda s, m: (m[0] ^ s, 0))
    return pl.pallas_call(
        functools.partial(norm_place_kernel, count),
        out_shape=[jax.ShapeDtypeStruct((count * rows, columns), jnp.bfloat16)] * 2,
        grid_spec=pltpu.PrefetchScalarGridSpec(
            num_scalar_prefetch=1,
            grid=(count,),
            in_specs=[whole((1, columns))] + [whole((rows, columns))] * count,
            out_specs=[spot, spot],
        ),
        compiler_params=params(14),
        cost_estimate=cost(0, 6 * count * rows * columns),
        name="norm_place",
    )(me, gain[None, :], *blocks)


def project_kernel(count, me, inputs, gain, *refs):
    attended, weight, normed, own = refs[:count], *refs[count:]
    joined = jnp.concatenate([a[...] for a in attended], axis=1)
    value = inputs[...].astype(jnp.float32) + dot(joined, weight[...], NN)
    recip = lax.rsqrt(jnp.mean(value * value, axis=-1, keepdims=True) + EPS)
    normed[...] = (value * recip * gain[...]).astype(jnp.bfloat16)

    @pl.when(pl.program_id(0) == me[0])
    def _():
        own[...] = value


def project(inputs, gain, attended, weight, me):
    count = len(attended)
    rows_all, columns = inputs.shape
    rows = rows_all // count
    depth = attended[0].shape[1]
    mine = pl.BlockSpec((rows, columns), lambda s, m: (s, 0))
    return pl.pallas_call(
        functools.partial(project_kernel, count),
        out_shape=[
            jax.ShapeDtypeStruct((rows_all, columns), jnp.bfloat16),
            jax.ShapeDtypeStruct((rows, columns), jnp.float32),
        ],
        grid_spec=pltpu.PrefetchScalarGridSpec(
            num_scalar_prefetch=1,
            grid=(count,),
            in_specs=[mine, whole((1, columns))]
            + [pl.BlockSpec((rows, depth), lambda s, m: (s, 0))] * count
            + [whole(weight.shape)],
            out_specs=[mine, pl.BlockSpec((rows, columns), lambda s, m: (0, 0))],
        ),
        compiler_params=params(30),
        cost_estimate=cost(
            2 * rows_all * depth * count * columns, 6 * inputs.size + 2 * weight.size
        ),
        name="project",
    )(me, inputs, gain[None, :], *attended, weight)


def swap(value, axis, size, bit):
    return lax.ppermute(value, axis, [(i, i ^ bit) for i in range(size)])


def gather_blocks(block, size):
    blocks = [block]
    for j in range(1, size):
        low = j & -j
        blocks.append(swap(blocks[j ^ low], "tensor", size, low))
    return blocks


def gather_weight(weight, size, dp):
    far = size // 2
    blocks = {0: weight}
    if dp % 2 == 0 and size >= 4:
        half = weight.shape[0] // 2
        side = lax.axis_index("dp") & 1
        part = lax.dynamic_slice(weight, (side * half, 0), (half, weight.shape[1]))
        part = swap(part, "tensor", size, far)
        other = swap(part, "dp", dp, 1)
        first, second = jnp.where(side == 0, part, other), jnp.where(side == 0, other, part)
        blocks[far] = jnp.concatenate([first, second], axis=0)
    for j in range(1, size):
        if j not in blocks:
            low = j & -j
            blocks[j] = swap(blocks[j ^ low], "tensor", size, low)
    return jnp.concatenate([blocks[j] for j in range(size)], axis=0)


def scatter_sum(array, size, me):
    rows = array.shape[0] // size
    parts = {
        j: lax.dynamic_slice(array, ((me ^ j) * rows, 0), (rows, array.shape[1]))
        for j in range(size)
    }
    bit = 1
    while bit < size:
        halves = {}
        for j in reversed(range(0, size, 2 * bit)):
            sent = swap(parts[j ^ bit].astype(jnp.bfloat16), "tensor", size, bit)
            halves[j] = parts[j].astype(jnp.float32) + sent.astype(jnp.float32)
        parts = halves
        bit *= 2
    return parts[0]


def after(value, *others):
    return lax.optimization_barrier((value, *others))[0]


def ring_order(size):
    return list(range(0, size, 2)) + list(reversed(range(1, size, 2)))


def slices_of(main, side, size, width):
    spans = [(0, main[0] // size, c) for c in range(0, main[1], width)]
    spans += [(1, side[0] // size, c) for c in range(0, side[1] // 2, width)]
    return spans, sum(span[1] for span in spans)


def pack_kernel(spans, width, start, main, side, out):
    at = 0
    for which, rows, column in spans:
        out[at : at + rows] = (main, side)[which][:, column : column + width]
        at += rows


def pack(main, side, half, start, sign, width, size):
    spans, depth = slices_of(main.shape, side.shape, size, width)

    def chunk(s, m):
        return lax.rem(m[0] + 2 * size - sign * (1 + s), size)

    return pl.pallas_call(
        functools.partial(pack_kernel, spans, width),
        out_shape=jax.ShapeDtypeStruct((size * depth, width), jnp.bfloat16),
        grid_spec=pltpu.PrefetchScalarGridSpec(
            num_scalar_prefetch=1,
            grid=(size,),
            in_specs=[
                pl.BlockSpec((main.shape[0] // size, main.shape[1]), lambda s, m: (chunk(s, m), 0)),
                pl.BlockSpec(
                    (side.shape[0] // size, side.shape[1] // 2), lambda s, m: (chunk(s, m), half)
                ),
            ],
            out_specs=pl.BlockSpec((depth, width), lambda s, m: (s, 0)),
        ),
        compiler_params=params(8),
        cost_estimate=cost(0, 4 * size * depth * width),
        name="pack",
    )(start, main, side)


def unpack_kernel(spans, width, count, start, *refs):
    pieces, outs = refs[: 2 * count], refs[-3:]
    for k in range(2 * count):

        @pl.when(pl.program_id(0) == k)
        def _(k=k):
            way, at = k // count, 0
            for which, rows, column in spans[way]:
                target = outs[2] if which else outs[way]
                value = pieces[k][at : at + rows].astype(jnp.float32)
                target[:, column : column + width] = value
                at += rows


def unpack(pieces, shapes, start, first, totals, width, size):
    spans = [slices_of(shape, shapes[2], size, width) for shape in shapes[:2]]
    depth = spans[0][1]
    count = len(pieces) // 2

    def forward(s, m):
        step = jnp.minimum(s, count - 1) + first
        return (lax.rem(m[0] + size - step, size), 0)

    def backward(s, m):
        step = jnp.maximum(s - count, 0) + first
        return (lax.rem(m[0] + step, size), 0)

    def beside(s, m):
        turned = s >= count
        chunk = jnp.where(turned, m[0] + s - count + first, m[0] + size - s - first)
        return (lax.rem(chunk, size), jnp.where(turned, 1, 0))

    held = [] if totals is None else list(totals)
    (rows_a, cols_a), (rows_b, cols_b), (rows_c, cols_c) = shapes
    return pl.pallas_call(
        functools.partial(unpack_kernel, [span[0] for span in spans], width, count),
        out_shape=[jax.ShapeDtypeStruct(shape, jnp.float32) for shape in shapes],
        grid_spec=pltpu.PrefetchScalarGridSpec(
            num_scalar_prefetch=1,
            grid=(2 * count,),
            in_specs=[whole((depth, width))] * (2 * count)
            + [pl.BlockSpec(memory_space=pl.ANY)] * len(held),
            out_specs=[
                pl.BlockSpec((rows_a // size, cols_a), forward),
                pl.BlockSpec((rows_b // size, cols_b), backward),
                pl.BlockSpec((rows_c // size, cols_c // 2), beside),
            ],
        ),
        input_output_aliases={1 + 2 * count + k: k for k in range(len(held))},
        compiler_params=params(56),
        cost_estimate=cost(0, 12 * count * depth * width),
        name="unpack",
    )(start, *pieces, *held)


def ring_sum(first, second, side, width, size):
    if size > 8:
        summed = lax.psum((first, second, side), "dp")
        return [total.astype(jnp.float32) for total in summed]
    order = ring_order(size)
    position = [0] * size
    for index, member in enumerate(order):
        position[member] = index
    start = jnp.array(position, jnp.int32)[lax.axis_index("dp")][None]
    hops = {
        sign: [(order[i], order[(i + sign) % size]) for i in range(size)] for sign in (1, -1)
    }

    def hop(k, value):
        return lax.ppermute(value, "dp", hops[(1, -1)[k]])

    packed = [
        pack(main, side, k, start, (1, -1)[k], width, size) for k, main in enumerate((first, second))
    ]
    depth = packed[0].shape[0] // size
    held = [array[:depth] for array in packed]
    for step in range(1, size):
        for k in range(2):
            moved = hop(k, held[k]).astype(jnp.float32)
            mine = packed[k][step * depth : (step + 1) * depth].astype(jnp.float32)
            held[k] = (moved + mine).astype(jnp.bfloat16)
    pieces = [[held[0]], [held[1]]]
    for _ in range(1, size):
        for k in range(2):
            pieces[k].append(hop(k, pieces[k][-1]))
    shapes = (first.shape, second.shape, side.shape)
    totals, low = None, 0
    for high in sorted({size // 2, size - 2, size - 1, size} - {0}):
        if high > low:
            some = pieces[0][low:high] + pieces[1][low:high]
            totals = unpack(some, shapes, start, low, totals, width, size)
            low = high
    return totals


def cross_sum(value, size, axis):
    if size & (size - 1) == 0:
        bit = 1
        while bit < size:
            value = value + swap(value, axis, size, bit)
            bit *= 2
        return value
    return lax.psum(value, axis)


def norm_backward(inputs, gain, dnormed):
    recip = lax.rsqrt(jnp.mean(inputs * inputs, axis=-1, keepdims=True) + EPS)
    scaled = gain * dnormed
    gain_part = jnp.sum(dnormed * inputs * recip, axis=0)
    inner = jnp.mean(scaled * inputs, axis=-1, keepdims=True)
    return (gain_part, recip * scaled - inputs * recip * recip * recip * inner)


def make_body(dp, tensor):
    def layer(
        block_input,
        gain_attention,
        gain_feedforward,
        w_query,
        w_key,
        w_value,
        w_output,
        w_gate,
        w_up,
        w_down,
        cotangent,
    ):
        pair_cols = w_key.shape[1]
        pairs = pair_cols // HD
        rows = block_input.shape[0]
        step = 256
        me = lax.axis_index("tensor")
        spot = me[None].astype(jnp.int32)
        cosine, sine = rope_tables(rows * tensor)
        w_padded = jnp.concatenate(
            [pad_halves(w_query), pad_halves(w_key), pad_heads(w_value)], axis=1
        )
        w_both = jnp.concatenate([w_key.T, w_value.T], axis=0)
        w_output_padded = pad_head_rows(w_output)

        blocks = gather_blocks(block_input, tensor)
        full_one, full_inputs = norm_place(blocks, gain_attention, spot)
        weight = gather_weight(after(w_output, blocks[-1]), tensor, dp)
        qkv = dot(full_one, w_padded, NN)
        heads, flat, q, k, v = attend(qkv, cosine, sine, pairs, step)
        attended = gather_blocks(flat, tensor)
        full_two, resid = project(full_inputs, gain_feedforward, attended, weight, spot)
        full_grad = place(gather_blocks(after(cotangent, attended[-1]), tensor), spot)

        gate = dot(full_two, w_gate, NN)
        up_proj = dot(full_two, w_up, NN)
        sigmoid_gate = jax.nn.sigmoid(gate)
        activated = gate * sigmoid_gate
        hidden = (activated * up_proj).astype(jnp.bfloat16)
        grad_down = dot(hidden, full_grad, TN).astype(jnp.bfloat16)
        dhidden = dot(full_grad, w_down, NT)
        dgate = (dhidden * up_proj * sigmoid_gate * (1.0 + gate * (1.0 - sigmoid_gate))).astype(
            jnp.bfloat16
        )
        dup_proj = (dhidden * activated).astype(jnp.bfloat16)
        grad_gate = dot(full_two, dgate, TN).astype(jnp.bfloat16)
        grad_up = dot(full_two, dup_proj, TN).astype(jnp.bfloat16)
        total_gate, total_up, total_down = ring_sum(grad_gate, grad_up, grad_down, 256, dp)
        dgate, dup_proj = lax.optimization_barrier((dgate, dup_proj, grad_gate, grad_up, grad_down))[:2]
        dnormed_two = (dot(dgate, w_gate, NT) + dot(dup_proj, w_up, NT)).astype(jnp.bfloat16)
        dnormed_two = scatter_sum(dnormed_two, tensor, me)
        gain_two_part, dresid_norm = norm_backward(resid, gain_feedforward, dnormed_two)
        dresid = cotangent.astype(jnp.float32) + dresid_norm
        full_dresid = place(gather_blocks(dresid.astype(jnp.bfloat16), tensor), spot)
        late_hidden = after(hidden, full_dresid)
        block_output = (
            resid
            + scatter_sum(dot(late_hidden, w_down, NN).astype(jnp.bfloat16), tensor, me)
        ).astype(jnp.bfloat16)
        dheads = dot(full_dresid, w_output_padded, NT).astype(jnp.bfloat16)
        dqkv = None
        for group in range(pairs):
            dqkv = attend_back(
                q, k, v, heads, dheads, cosine, sine, pairs, step, group, dqkv
            )
        grad_output = dot(flat, full_dresid, TN).astype(jnp.bfloat16)
        dquery, dboth = dqkv[:, : 2 * pair_cols], dqkv[:, 2 * pair_cols :]
        grad_query = dot(full_one, dquery, TN).astype(jnp.bfloat16)
        grad_both = dot(dboth, full_one, TN).astype(jnp.bfloat16)
        total_query, total_both, total_output = ring_sum(
            grad_query, grad_both, grad_output, w_query.shape[1], dp
        )
        dnormed_one = scatter_sum(
            (dot(dquery, w_query, NT) + dot(dboth, w_both, NN)).astype(jnp.bfloat16), tensor, me
        )
        gain_one_part, dinput_norm = norm_backward(
            block_input.astype(jnp.float32), gain_attention, dnormed_one
        )
        input_grad = (dresid + dinput_norm).astype(jnp.bfloat16)
        gains = jnp.stack([gain_one_part, gain_two_part])
        gains = cross_sum(cross_sum(gains, tensor, "tensor"), dp, "dp")
        return (
            block_output,
            input_grad,
            gains[0],
            gains[1],
            total_query,
            total_both[:pair_cols].T,
            total_both[pair_cols:].T,
            total_output,
            total_gate,
            total_up,
            total_down,
        )

    return layer


def solution(mesh):
    placed = (
        P(("dp", "tensor"), None),
        P(),
        P(),
        P(None, "tensor"),
        P(None, "tensor"),
        P(None, "tensor"),
        P("tensor", None),
        P(None, "tensor"),
        P(None, "tensor"),
        P("tensor", None),
        P(("dp", "tensor"), None),
    )
    return jax.shard_map(
        make_body(mesh.shape["dp"], mesh.shape["tensor"]),
        mesh=mesh,
        in_specs=placed,
        out_specs=(
            P(("dp", "tensor"), None),
            P(("dp", "tensor"), None),
            P(),
            P(),
            P(None, "tensor"),
            P(None, "tensor"),
            P(None, "tensor"),
            P("tensor", None),
            P(None, "tensor"),
            P(None, "tensor"),
            P("tensor", None),
        ),
        check_vma=False,
    )
```

profile of v0, /device:TPU:0, one launch (start us, length us, event | category | flops | bytes accessed | tf_op | source)
XLA Modules:
  0.0 497.2 jit_solution(16646920556429779842)
XLA Ops:
  3.7 17.9 %collective-permute-done.1.refs_2_ = bf16[256,1536]{1,0:T(8,128)(2,1)} collective-permute-done((bf16[256,1536]{1,0:T(8,128)(2,1)}, bf16[256,1536]{1,0:T(8,128)(2,1)}, u32[]{:S(2)}, u32[]{:S(2)}) %collective-permute-start.1) | collective-permute-done | bytes 786464 | tf_op jit(solution)/shard_map/ppermute | solution.py:308
  52.5 7.8 %attend.1 = (bf16[1024,512]{1,0:T(8,128)(2,1)S(1)}, bf16[1024,384]{1,0:T(8,128)(2,1)}, bf16[1024,512]{1,0:T(8,128)(2,1)S(1)}, bf16[1024,256]{1,0:T(8,128)(2,1)S(1)}, bf16[1024,256]{1,0:T(8,128)(2,1)S(1)}) custom-call(f32[1024,1024]{1,0:T(8,128)S(1)} %fusion.1.qkv, f32[1024,128]{1,0:T(8,128)S(1)} %get-tuple-element.114.cosine.refs_5_, ...), custom_call_target="tpu_custom_call" | custom-call | flops 1342177280 | bytes 10485760 | tf_op jit(solution)/shard_map/attend/pallas_call | solution.py:138
  68.7 10.8 %collective-permute-done.4.refs_2_ = bf16[1024,384]{1,0:T(8,128)(2,1)} collective-permute-done((bf16[1024,384]{1,0:T(8,128)(2,1)}, bf16[1024,384]{1,0:T(8,128)(2,1)}, u32[]{:S(2)}, u32[]{:S(2)}) %collective-permute-start.4) | collective-permute-done | bytes 786464 | tf_op jit(solution)/shard_map/ppermute | solution.py:308
  86.3 9.5 %project.1 = (bf16[1024,1536]{1,0:T(8,128)(2,1)S(1)}, f32[256,1536]{1,0:T(8,128)S(1)}) custom-call(s32[1]{0:T(128)} %bitcast.me, bf16[1024,1536]{1,0:T(8,128)(2,1)S(1)} %copy-done.19, f32[1,1536]{1,0:T(1,128)S(1)} %broadcast_in_dim.8.gain, bf16[1024,384]{1,0:T(8,128)(2,1)} %get-tuple-element.51.refs_0_, bf16[1024,384]{1,0:T(8,128)(2,1)} %collective-permute-done.3.refs_1_, ...), custom_call_target="tpu_custom_call" | custom-call | flops 4831838208 | bytes 14155776 | tf_op jit(solution)/shard_map/project/pallas_call | solution.py:285
  107.4 9.2 %multiply_convert_fusion = (bf16[1024,1024]{1,0:T(8,128)(2,1)}, bf16[1024,1024]{1,0:T(8,128)(2,1)}, bf16[1024,1024]{1,0:T(8,128)(2,1)}) fusion(f32[1024,1024]{1,0:T(8,128)} %fusion.33, f32[1024,1024]{1,0:T(8,128)} %fusion.34, bf16[1024,1536]{1,0:T(8,128)(2,1)S(1)} %place.2, bf16[1024,1536]{1,0:T(8,128)(2,1)S(1)} %copy-done), kind=kOutput, calls=%fused_computation.2 | convolution fusion | flops 3236954112 | bytes 20971520 | tf_op jit(solution)/shard_map/dot_general | solution.py:62
  140.1 6.3 %add_convert_fusion.1 = bf16[1024,1536]{1,0:T(8,128)(2,1)S(1)} fusion(f32[1024,1536]{1,0:T(8,128)} %fusion.35, bf16[1024,1024]{1,0:T(8,128)(2,1)} %get-tuple-element.57, bf16[1536,1024]{1,0:T(8,128)(2,1)S(1)} %copy-done.62), kind=kOutput, calls=%fused_computation.1 | convolution fusion | flops 3224371200 | bytes 14680064 | tf_op jit(solution)/shard_map/dot_general | solution.py:62
  147.1 6.7 %collective-permute-done.72 = bf16[1152,256]{1,0:T(8,128)(2,1)S(1)} collective-permute-done((bf16[1152,256]{1,0:T(8,128)(2,1)S(1)}, bf16[1152,256]{1,0:T(8,128)(2,1)S(1)}, u32[]{:S(2)}, u32[]{:S(2)}) %collective-permute-start.72) | collective-permute-done | bytes 589856 | tf_op jit(solution)/shard_map/ppermute | solution.py:470
  158.1 10.8 %collective-permute-done.73 = bf16[1152,256]{1,0:T(8,128)(2,1)S(1)} collective-permute-done((bf16[1152,256]{1,0:T(8,128)(2,1)S(1)}, bf16[1152,256]{1,0:T(8,128)(2,1)S(1)}, u32[]{:S(2)}, u32[]{:S(2)}) %collective-permute-start.73) | collective-permute-done | bytes 589856 | tf_op jit(solution)/shard_map/ppermute | solution.py:470
  175.9 7.3 %collective-permute-done.74 = bf16[1152,256]{1,0:T(8,128)(2,1)S(1)} collective-permute-done((bf16[1152,256]{1,0:T(8,128)(2,1)S(1)}, bf16[1152,256]{1,0:T(8,128)(2,1)S(1)}, u32[]{:S(2)}, u32[]{:S(2)}) %collective-permute-start.74) | collective-permute-done | bytes 589856 | tf_op jit(solution)/shard_map/ppermute | solution.py:470
  188.1 8.6 %collective-permute-done.75 = bf16[1152,256]{1,0:T(8,128)(2,1)S(1)} collective-permute-done((bf16[1152,256]{1,0:T(8,128)(2,1)S(1)}, bf16[1152,256]{1,0:T(8,128)(2,1)S(1)}, u32[]{:S(2)}, u32[]{:S(2)}) %collective-permute-start.75) | collective-permute-done | bytes 589856 | tf_op jit(solution)/shard_map/ppermute | solution.py:470
  203.4 5.8 %collective-permute-done.76 = bf16[1152,256]{1,0:T(8,128)(2,1)S(1)} collective-permute-done((bf16[1152,256]{1,0:T(8,128)(2,1)S(1)}, bf16[1152,256]{1,0:T(8,128)(2,1)S(1)}, u32[]{:S(2)}, u32[]{:S(2)}) %collective-permute-start.76) | collective-permute-done | bytes 589856 | tf_op jit(solution)/shard_map/ppermute | solution.py:470
  218.4 6.5 %attend_back.2.refs_7_ = bf16[1024,768]{1,0:T(8,128)(2,1)S(1)} custom-call(bf16[1024,512]{1,0:T(8,128)(2,1)S(1)} %copy-done.10, bf16[1024,256]{1,0:T(8,128)(2,1)S(1)} %copy-done.13, bf16[1024,256]{1,0:T(8,128)(2,1)S(1)} %copy-done.15, bf16[1024,512]{1,0:T(8,128)(2,1)S(1)} %copy-done.8, bf16[1024,512]{1,0:T(8,128)(2,1)S(1)} %convolution_convert_fusion.7.refs_4_, ...), custom_call_target="tpu_custom_call" | custom-call | flops 1677721600 | bytes 5242880 | tf_op jit(solution)/shard_map/attend_back/pallas_call | solution.py:197
  224.9 6.7 %attend_back.3 = bf16[1024,768]{1,0:T(8,128)(2,1)S(1)} custom-call(bf16[1024,512]{1,0:T(8,128)(2,1)S(1)} %copy-done.10, bf16[1024,256]{1,0:T(8,128)(2,1)S(1)} %copy-done.13, bf16[1024,256]{1,0:T(8,128)(2,1)S(1)} %copy-done.15, bf16[1024,512]{1,0:T(8,128)(2,1)S(1)} %copy-done.8, bf16[1024,512]{1,0:T(8,128)(2,1)S(1)} %convolution_convert_fusion.7.refs_4_, ...), custom_call_target="tpu_custom_call" | custom-call | flops 1677721600 | bytes 5242880 | tf_op jit(solution)/shard_map/attend_back/pallas_call | solution.py:197
  279.4 13.6 %collective-permute-done.47 = bf16[288,384]{1,0:T(8,128)(2,1)S(1)} collective-permute-done((bf16[288,384]{1,0:T(8,128)(2,1)S(1)}, bf16[288,384]{1,0:T(8,128)(2,1)S(1)}, u32[]{:S(2)}, u32[]{:S(2)}) %collective-permute-start.47) | collective-permute-done | bytes 221216 | tf_op jit(solution)/shard_map/ppermute | solution.py:470
  293.9 7.4 %collective-permute-done.33 = bf16[288,384]{1,0:T(8,128)(2,1)S(1)} collective-permute-done((bf16[288,384]{1,0:T(8,128)(2,1)S(1)}, bf16[288,384]{1,0:T(8,128)(2,1)S(1)}, u32[]{:S(2)}, u32[]{:S(2)}) %collective-permute-start.33) | collective-permute-done | bytes 221216 | tf_op jit(solution)/shard_map/ppermute | solution.py:470
  304.1 7.1 %collective-permute-done.64 = bf16[1152,256]{1,0:T(8,128)(2,1)S(1)} collective-permute-done((bf16[1152,256]{1,0:T(8,128)(2,1)S(1)}, bf16[1152,256]{1,0:T(8,128)(2,1)S(1)}, u32[]{:S(2)}, u32[]{:S(2)}) %collective-permute-start.64) | collective-permute-done | bytes 589856 | tf_op jit(solution)/shard_map/ppermute | solution.py:470
  324.1 7.1 %collective-permute-done.49 = bf16[288,384]{1,0:T(8,128)(2,1)S(1)} collective-permute-done((bf16[288,384]{1,0:T(8,128)(2,1)S(1)}, bf16[288,384]{1,0:T(8,128)(2,1)S(1)}, u32[]{:S(2)}, u32[]{:S(2)}) %collective-permute-start.49) | collective-permute-done | bytes 221216 | tf_op jit(solution)/shard_map/ppermute | solution.py:470
  334.6 9.2 %collective-permute-done.35 = bf16[288,384]{1,0:T(8,128)(2,1)S(1)} collective-permute-done((bf16[288,384]{1,0:T(8,128)(2,1)S(1)}, bf16[288,384]{1,0:T(8,128)(2,1)S(1)}, u32[]{:S(2)}, u32[]{:S(2)}) %collective-permute-start.35) | collective-permute-done | bytes 221216 | tf_op jit(solution)/shard_map/ppermute | solution.py:470
  357.7 6.7 %collective-permute-done.80.refs_6_ = bf16[1152,256]{1,0:T(8,128)(2,1)S(1)} collective-permute-done((bf16[1152,256]{1,0:T(8,128)(2,1)S(1)}, bf16[1152,256]{1,0:T(8,128)(2,1)S(1)}, u32[]{:S(2)}, u32[]{:S(2)}) %collective-permute-start.80) | collective-permute-done | bytes 589856 | tf_op jit(solution)/shard_map/ppermute | solution.py:470
  368.8 11.7 %collective-permute-done.27 = f32[2,1536]{1,0:T(2,128)S(1)} collective-permute-done((f32[2,1536]{1,0:T(2,128)S(1)}, f32[2,1536]{1,0:T(2,128)S(1)}, u32[]{:S(2)}, u32[]{:S(2)}) %collective-permute-start.27) | collective-permute-done | bytes 12320 | tf_op jit(solution)/shard_map/ppermute | solution.py:308
  388.8 12.6 %collective-permute-done.52.refs_6_ = bf16[288,384]{1,0:T(8,128)(2,1)S(1)} collective-permute-done((bf16[288,384]{1,0:T(8,128)(2,1)S(1)}, bf16[288,384]{1,0:T(8,128)(2,1)S(1)}, u32[]{:S(2)}, u32[]{:S(2)}) %collective-permute-start.52) | collective-permute-done | bytes 221216 | tf_op jit(solution)/shard_map/ppermute | solution.py:470
  418.4 12.2 %collective-permute-done.55.refs_3_ = bf16[288,384]{1,0:T(8,128)(2,1)S(1)} collective-permute-done((bf16[288,384]{1,0:T(8,128)(2,1)S(1)}, bf16[288,384]{1,0:T(8,128)(2,1)S(1)}, u32[]{:S(2)}, u32[]{:S(2)}) %collective-permute-start.55) | collective-permute-done | bytes 221216 | tf_op jit(solution)/shard_map/ppermute | solution.py:470
  442.7 10.6 %collective-permute-done.29 = f32[2,1536]{1,0:T(2,128)S(1)} collective-permute-done((f32[2,1536]{1,0:T(2,128)S(1)}, f32[2,1536]{1,0:T(2,128)S(1)}, u32[]{:S(2)}, u32[]{:S(2)}) %collective-permute-start.29) | collective-permute-done | bytes 12320 | tf_op jit(solution)/shard_map/ppermute | solution.py:308
  466.0 8.1 %unpack.12 = (f32[1536,1024]{1,0:T(8,128)}, f32[1536,1024]{1,0:T(8,128)}, f32[1024,1536]{1,0:T(8,128)}) custom-call(s32[1]{0:T(128)} %dynamic_slice.58.start, bf16[1152,256]{1,0:T(8,128)(2,1)} %copy-done.28, bf16[1152,256]{1,0:T(8,128)(2,1)} %copy-done.35, bf16[1152,256]{1,0:T(8,128)(2,1)} %copy-done.37, bf16[1152,256]{1,0:T(8,128)(2,1)} %copy-done.39, ...), custom_call_target="tpu_custom_call" | custom-call | bytes 14155776 | tf_op jit(solution)/shard_map/unpack/pallas_call | solution.py:435
  (399 shorter events, 274.5 us)
Async XLA Ops:
  0.7 20.9 %collective-permute-start.1 = (bf16[256,1536]{1,0:T(8,128)(2,1)}, bf16[256,1536]{1,0:T(8,128)(2,1)}, u32[]{:S(2)}, u32[]{:S(2)}) collective-permute-start(bf16[256,1536]{1,0:T(8,128)(2,1)} %refs_0_.1), channel_id=1, source_target_pairs={{0,2},{1,3},{2,0},{3,1},{4,6},{5,7},{6,4},{7,5},{8,10},{9,11},{10,... | collective-permute-start | bytes 2359304 | tf_op jit(solution)/shard_map/ppermute | solution.py:308
  34.9 28.1 %collective-permute-start.6 = (bf16[384,1536]{1,0:T(8,128)(2,1)S(1)}, bf16[384,1536]{1,0:T(8,128)(2,1)S(1)}, u32[]{:S(2)}, u32[]{:S(2)}) collective-permute-start(bf16[384,1536]{1,0:T(8,128)(2,1)S(1)} %copy-done.20), channel_id=1, source_target_pairs={{0,1},{1,0},{2,3},{3,2},{4,5},{5,4},{6,7},{7,6},{8,9},{9,8},{10,11... | collective-permute-start | bytes 3538952 | tf_op jit(solution)/shard_map/ppermute | solution.py:308
  82.4 19.7 %collective-permute-start.11 = (bf16[256,1536]{1,0:T(8,128)(2,1)}, bf16[256,1536]{1,0:T(8,128)(2,1)S(1)}, u32[]{:S(2)}, u32[]{:S(2)}) collective-permute-start(bf16[256,1536]{1,0:T(8,128)(2,1)} %refs_0_.2), channel_id=1, source_target_pairs={{0,2},{1,3},{2,0},{3,1},{4,6},{5,7},{6,4},{7,5},{8,10},{9,11},{10,... | collective-permute-start | bytes 2359304 | tf_op jit(solution)/shard_map/ppermute | solution.py:308
  84.0 23.1 %collective-permute-start.10 = (bf16[256,1536]{1,0:T(8,128)(2,1)}, bf16[256,1536]{1,0:T(8,128)(2,1)S(1)}, u32[]{:S(2)}, u32[]{:S(2)}) collective-permute-start(bf16[256,1536]{1,0:T(8,128)(2,1)} %refs_0_.2), channel_id=1, source_target_pairs={{0,1},{1,0},{2,3},{3,2},{4,5},{5,4},{6,7},{7,6},{8,9},{9,8},{10,11... | collective-permute-start | bytes 2359304 | tf_op jit(solution)/shard_map/ppermute | solution.py:308
  146.6 24.9 %collective-permute-start.13 = (bf16[256,1536]{1,0:T(8,128)(2,1)S(1)}, bf16[256,1536]{1,0:T(8,128)(2,1)S(1)}, u32[]{:S(2)}, u32[]{:S(2)}) collective-permute-start(bf16[256,1536]{1,0:T(8,128)(2,1)S(1)} %get-tuple-element.106), channel_id=1, source_target_pairs={{0,1},{1,0},{2,3},{3,2},{4,5},{5,4},{6,7},{7,6},{8,9},{9,8},{10,11... | collective-permute-start | bytes 2359304 | tf_op jit(solution)/shard_map/ppermute | solution.py:308
  210.2 39.3 %collective-permute-start.77 = (bf16[1152,256]{1,0:T(8,128)(2,1)}, bf16[1152,256]{1,0:T(8,128)(2,1)S(1)}, u32[]{:S(2)}, u32[]{:S(2)}) collective-permute-start(bf16[1152,256]{1,0:T(8,128)(2,1)} %add_convert_fusion.8), channel_id=1, source_target_pairs={{0,4},{8,0},{16,8},{24,16},{28,24},{20,28},{12,20},{4,12},{1,5},{9... | collective-permute-start | bytes 1769480 | tf_op jit(solution)/shard_map/ppermute | solution.py:470
  211.4 38.4 %collective-permute-start.63 = (bf16[1152,256]{1,0:T(8,128)(2,1)}, bf16[1152,256]{1,0:T(8,128)(2,1)}, u32[]{:S(2)}, u32[]{:S(2)}) collective-permute-start(bf16[1152,256]{1,0:T(8,128)(2,1)} %add_convert_fusion.15), channel_id=1, source_target_pairs={{0,8},{8,16},{16,24},{24,28},{28,20},{20,12},{12,4},{4,0},{1,9},{9... | collective-permute-start | bytes 1769480 | tf_op jit(solution)/shard_map/ppermute | solution.py:470
  246.1 122.1 %collective-permute-start.19 = (bf16[256,1536]{1,0:T(8,128)(2,1)}, bf16[256,1536]{1,0:T(8,128)(2,1)S(1)}, u32[]{:S(2)}, u32[]{:S(2)}) collective-permute-start(bf16[256,1536]{1,0:T(8,128)(2,1)} %get-tuple-element.104), channel_id=1, source_target_pairs={{0,1},{1,0},{2,3},{3,2},{4,5},{5,4},{6,7},{7,6},{8,9},{9,8},{10,11... | collective-permute-start | bytes 2359304 | tf_op jit(solution)/shard_map/ppermute | solution.py:308
  248.8 155.3 %collective-permute-start.20 = (bf16[256,1536]{1,0:T(8,128)(2,1)}, bf16[256,1536]{1,0:T(8,128)(2,1)S(1)}, u32[]{:S(2)}, u32[]{:S(2)}) collective-permute-start(bf16[256,1536]{1,0:T(8,128)(2,1)} %get-tuple-element.105), channel_id=1, source_target_pairs={{0,1},{1,0},{2,3},{3,2},{4,5},{5,4},{6,7},{7,6},{8,9},{9,8},{10,11... | collective-permute-start | bytes 2359304 | tf_op jit(solution)/shard_map/ppermute | solution.py:308
  249.1 82.4 %collective-permute-start.22 = (bf16[256,1536]{1,0:T(8,128)(2,1)S(1)}, bf16[256,1536]{1,0:T(8,128)(2,1)S(1)}, u32[]{:S(2)}, u32[]{:S(2)}) collective-permute-start(bf16[256,1536]{1,0:T(8,128)(2,1)S(1)} %get-tuple-element.102), channel_id=1, source_target_pairs={{0,1},{1,0},{2,3},{3,2},{4,5},{5,4},{6,7},{7,6},{8,9},{9,8},{10,11... | collective-permute-start | bytes 2359304 | tf_op jit(solution)/shard_map/ppermute | solution.py:308
  249.5 28.0 %collective-permute-start.23 = (bf16[256,1536]{1,0:T(8,128)(2,1)S(1)}, bf16[256,1536]{1,0:T(8,128)(2,1)S(1)}, u32[]{:S(2)}, u32[]{:S(2)}) collective-permute-start(bf16[256,1536]{1,0:T(8,128)(2,1)S(1)} %get-tuple-element.103), channel_id=1, source_target_pairs={{0,1},{1,0},{2,3},{3,2},{4,5},{5,4},{6,7},{7,6},{8,9},{9,8},{10,11... | collective-permute-start | bytes 2359304 | tf_op jit(solution)/shard_map/ppermute | solution.py:308
  276.4 25.8 %collective-permute-start.78 = (bf16[1152,256]{1,0:T(8,128)(2,1)S(1)}, bf16[1152,256]{1,0:T(8,128)(2,1)S(1)}, u32[]{:S(2)}, u32[]{:S(2)}) collective-permute-start(bf16[1152,256]{1,0:T(8,128)(2,1)S(1)} %add_convert_fusion.7), channel_id=1, source_target_pairs={{0,4},{8,0},{16,8},{24,16},{28,24},{20,28},{12,20},{4,12},{1,5},{9... | collective-permute-start | bytes 1769480 | tf_op jit(solution)/shard_map/ppermute | solution.py:470
  302.2 31.1 %collective-permute-start.24 = (bf16[256,1536]{1,0:T(8,128)(2,1)S(1)}, bf16[256,1536]{1,0:T(8,128)(2,1)S(1)}, u32[]{:S(2)}, u32[]{:S(2)}) collective-permute-start(bf16[256,1536]{1,0:T(8,128)(2,1)S(1)} %add_convert_fusion.2), channel_id=1, source_target_pairs={{0,2},{1,3},{2,0},{3,1},{4,6},{5,7},{6,4},{7,5},{8,10},{9,11},{10,... | collective-permute-start | bytes 2359304 | tf_op jit(solution)/shard_map/ppermute | solution.py:308
  380.7 29.4 %collective-permute-start.82 = (bf16[1152,256]{1,0:T(8,128)(2,1)S(1)}, bf16[1152,256]{1,0:T(8,128)(2,1)S(1)}, u32[]{:S(2)}, u32[]{:S(2)}) collective-permute-start(bf16[1152,256]{1,0:T(8,128)(2,1)S(1)} %collective-permute-done.81.refs_7_), channel_id=1, source_target_pairs={{0,4},{8,0},{16,8},{24,16},{28,24},{20,28},{12,20},{4,12},{1,5},{9... | collective-permute-start | bytes 1769480 | tf_op jit(solution)/shard_map/ppermute | solution.py:470
  382.6 29.5 %collective-permute-start.68 = (bf16[1152,256]{1,0:T(8,128)(2,1)S(1)}, bf16[1152,256]{1,0:T(8,128)(2,1)S(1)}, u32[]{:S(2)}, u32[]{:S(2)}) collective-permute-start(bf16[1152,256]{1,0:T(8,128)(2,1)S(1)} %collective-permute-done.67.refs_3_), channel_id=1, source_target_pairs={{0,8},{8,16},{16,24},{24,28},{28,20},{20,12},{12,4},{4,0},{1,9},{9... | collective-permute-start | bytes 1769480 | tf_op jit(solution)/shard_map/ppermute | solution.py:470
  410.1 22.6 %collective-permute-start.83 = (bf16[1152,256]{1,0:T(8,128)(2,1)S(1)}, bf16[1152,256]{1,0:T(8,128)(2,1)S(1)}, u32[]{:S(2)}, u32[]{:S(2)}) collective-permute-start(bf16[1152,256]{1,0:T(8,128)(2,1)S(1)} %collective-permute-done.82.refs_2_), channel_id=1, source_target_pairs={{0,4},{8,0},{16,8},{24,16},{28,24},{20,28},{12,20},{4,12},{1,5},{9... | collective-permute-start | bytes 1769480 | tf_op jit(solution)/shard_map/ppermute | solution.py:470
  412.1 22.4 %collective-permute-start.69 = (bf16[1152,256]{1,0:T(8,128)(2,1)S(1)}, bf16[1152,256]{1,0:T(8,128)(2,1)S(1)}, u32[]{:S(2)}, u32[]{:S(2)}) collective-permute-start(bf16[1152,256]{1,0:T(8,128)(2,1)S(1)} %collective-permute-done.68.refs_0_), channel_id=1, source_target_pairs={{0,8},{8,16},{16,24},{24,28},{28,20},{20,12},{12,4},{4,0},{1,9},{9... | collective-permute-start | bytes 1769480 | tf_op jit(solution)/shard_map/ppermute | solution.py:470
  412.4 24.2 %collective-permute-start.21 = (bf16[256,1536]{1,0:T(8,128)(2,1)S(1)}, bf16[256,1536]{1,0:T(8,128)(2,1)S(1)}, u32[]{:S(2)}, u32[]{:S(2)}) collective-permute-start(bf16[256,1536]{1,0:T(8,128)(2,1)S(1)} %add_convert_fusion.4), channel_id=1, source_target_pairs={{0,2},{1,3},{2,0},{3,1},{4,6},{5,7},{6,4},{7,5},{8,10},{9,11},{10,... | collective-permute-start | bytes 2359304 | tf_op jit(solution)/shard_map/ppermute | solution.py:308
  432.7 20.5 %collective-permute-start.84 = (bf16[1152,256]{1,0:T(8,128)(2,1)S(1)}, bf16[1152,256]{1,0:T(8,128)(2,1)S(1)}, u32[]{:S(2)}, u32[]{:S(2)}) collective-permute-start(bf16[1152,256]{1,0:T(8,128)(2,1)S(1)} %collective-permute-done.83.refs_3_), channel_id=1, source_target_pairs={{0,4},{8,0},{16,8},{24,16},{28,24},{20,28},{12,20},{4,12},{1,5},{9... | collective-permute-start | bytes 1769480 | tf_op jit(solution)/shard_map/ppermute | solution.py:470
  434.6 21.1 %collective-permute-start.70 = (bf16[1152,256]{1,0:T(8,128)(2,1)S(1)}, bf16[1152,256]{1,0:T(8,128)(2,1)}, u32[]{:S(2)}, u32[]{:S(2)}) collective-permute-start(bf16[1152,256]{1,0:T(8,128)(2,1)S(1)} %collective-permute-done.69.refs_1_), channel_id=1, source_target_pairs={{0,8},{8,16},{16,24},{24,28},{28,20},{20,12},{12,4},{4,0},{1,9},{9... | collective-permute-start | bytes 1769480 | tf_op jit(solution)/shard_map/ppermute | solution.py:470
  439.3 37.5 %collective-permute-start.57 = (bf16[288,384]{1,0:T(8,128)(2,1)}, bf16[288,384]{1,0:T(8,128)(2,1)S(1)}, u32[]{:S(2)}, u32[]{:S(2)}) collective-permute-start(bf16[288,384]{1,0:T(8,128)(2,1)} %collective-permute-done.56.refs_1_), channel_id=1, source_target_pairs={{0,4},{8,0},{16,8},{24,16},{28,24},{20,28},{12,20},{4,12},{1,5},{9... | collective-permute-start | bytes 663560 | tf_op jit(solution)/shard_map/ppermute | solution.py:470
  440.9 35.9 %collective-permute-start.43 = (bf16[288,384]{1,0:T(8,128)(2,1)}, bf16[288,384]{1,0:T(8,128)(2,1)S(1)}, u32[]{:S(2)}, u32[]{:S(2)}) collective-permute-start(bf16[288,384]{1,0:T(8,128)(2,1)} %collective-permute-done.42.refs_0_), channel_id=1, source_target_pairs={{0,8},{8,16},{16,24},{24,28},{28,20},{20,12},{12,4},{4,0},{1,9},{9... | collective-permute-start | bytes 663560 | tf_op jit(solution)/shard_map/ppermute | solution.py:470
  453.2 39.0 %collective-permute-start.85 = (bf16[1152,256]{1,0:T(8,128)(2,1)S(1)}, bf16[1152,256]{1,0:T(8,128)(2,1)S(1)}, u32[]{:S(2)}, u32[]{:S(2)}) collective-permute-start(bf16[1152,256]{1,0:T(8,128)(2,1)S(1)} %collective-permute-done.84.refs_1_), channel_id=1, source_target_pairs={{0,4},{8,0},{16,8},{24,16},{28,24},{20,28},{12,20},{4,12},{1,5},{9... | collective-permute-start | bytes 1769480 | tf_op jit(solution)/shard_map/ppermute | solution.py:470
  455.7 36.5 %collective-permute-start.71 = (bf16[1152,256]{1,0:T(8,128)(2,1)}, bf16[1152,256]{1,0:T(8,128)(2,1)S(1)}, u32[]{:S(2)}, u32[]{:S(2)}) collective-permute-start(bf16[1152,256]{1,0:T(8,128)(2,1)} %collective-permute-done.70.refs_0_), channel_id=1, source_target_pairs={{0,8},{8,16},{16,24},{24,28},{28,20},{20,12},{12,4},{4,0},{1,9},{9... | collective-permute-start | bytes 1769480 | tf_op jit(solution)/shard_map/ppermute | solution.py:470
  (130 other events, 2116.0 us)
where the time goes:
time: 502 us; the launch traced here: 497 us
  waiting for transfers between devices  234 us (47%)
  starting transfers between devices  79.4 us (16%)
  Pallas kernels  75.2 us (15%)
  matrix products  62.5 us (12%)
  local copies, waits for them, and re-layouts  25.2 us (5%)
  other arithmetic  18.9 us (4%)
    ppermute x56, waiting for transfers between devices, hop(): return lax.ppermute(value, 'dp', hops[(1, -1)[k]])  165 us
    ppermute x30, waiting for transfers between devices, swap(): return lax.ppermute(value, axis, [(i, i ^ bit) for i in range(size)])  69 us
    dot_general x16, matrix products, dot(): lax.dot_general(left, right, (dims, ((), ())), preferred_element_type=jnp...  62.5 us
    ppermute x56, starting transfers between devices, hop(): return lax.ppermute(value, 'dp', hops[(1, -1)[k]])  54.2 us
    pallas_call x8, Pallas kernels, unpack(): pl.pallas_call(functools.partial(unpack_kernel, [span[0] for span in span...  35.4 us
    ppermute x30, starting transfers between devices, swap(): return lax.ppermute(value, axis, [(i, i ^ bit) for i in range(size)])  25.1 us
    pallas_call x2, Pallas kernels, attend_back(): pl.pallas_call(functools.partial(attend_back_kernel, pairs, step, group),...  13.2 us
  transfers between devices with their start and end apart: 86, of which 43 were waited for; matrix products, arithmetic and copies ran while one was open for 15% of the time, Pallas kernels for 14%

commit v1 on v0

--- a/solution.py
+++ b/solution.py
@@ -98,8 +98,7 @@
     return value * cosine + pltpu.roll(value * sine, LANES // 2, 1)
 
 
-def attend_kernel(pairs, step, qkv, cosine, sine, heads_out, flat_out, q_out, k_out, v_out):
-    rows = cosine.shape[0]
+def turn_kernel(pairs, qkv, cosine, sine, q_out, k_out, v_out):
     cos, sin = cosine[...], sine[...]
     for h in range(2 * pairs):
         q_out[:, h * LANES : (h + 1) * LANES] = turn(
@@ -112,18 +111,30 @@
         ).astype(jnp.bfloat16)
     at = 3 * pairs * LANES
     v_out[...] = qkv[:, at : at + pairs * LANES].astype(jnp.bfloat16)
+
+
+def attend_kernel(pairs, step, part, *refs):
+    heads_out, flat_out = refs[-5:-3] if part == 0 else refs[-2:]
+    if part == 0:
+        turn_kernel(pairs, *refs[:3], *refs[-3:])
+        q, k, v = refs[-3:]
+    else:
+        q, k, v = refs[:3]
+    rows = q.shape[0]
+    low = part * (rows // 2)
     for g in range(pairs):
         kv = slice(g * LANES, (g + 1) * LANES)
-        for block in range(rows // step):
+        for block in range(low // step, (low + rows // 2) // step):
             here = slice(block * step, (block + 1) * step)
+            there = slice(block * step - low, (block + 1) * step - low)
             start = (block * step) // L * L
             past = slice(start, (block + 1) * step)
             one, two = (slice((2 * g + e) * LANES, (2 * g + e + 1) * LANES) for e in range(2))
-            query = jnp.concatenate([q_out[here, one], q_out[here, two]], axis=0)
-            prob = softmax_block(query, k_out[past, kv], block, step, start).astype(jnp.bfloat16)
-            result = dot(prob, v_out[past, kv], NN).astype(jnp.bfloat16)
-            heads_out[here, one] = result[:step]
-            heads_out[here, two] = result[step:]
+            query = jnp.concatenate([q[here, one], q[here, two]], axis=0)
+            prob = softmax_block(query, k[past, kv], block, step, start).astype(jnp.bfloat16)
+            result = dot(prob, v[past, kv], NN).astype(jnp.bfloat16)
+            heads_out[there, one] = result[:step]
+            heads_out[there, two] = result[step:]
     flat = sum(
         dot(heads_out[:, h * LANES : (h + 1) * LANES], selection(2 * pairs * HD, h, False), NN)
         for h in range(2 * pairs)
@@ -131,21 +142,23 @@
     flat_out[...] = flat.astype(jnp.bfloat16)
 
 
-def attend(qkv, cosine, sine, pairs, step):
-    rows = qkv.shape[0]
-    shapes = [2 * pairs * LANES, 2 * pairs * HD, 2 * pairs * LANES, pairs * LANES, pairs * LANES]
-    area = rows * min(rows, L) * 2 * pairs * 5 // 8
+def attend(inputs, pairs, step, part):
+    rows = inputs[0].shape[0]
+    shapes = [(rows // 2, 2 * pairs * LANES), (rows // 2, 2 * pairs * HD)]
+    if part == 0:
+        shapes += [(rows, 2 * pairs * LANES), (rows, pairs * LANES), (rows, pairs * LANES)]
+    area = rows * min(rows, L) * 2 * pairs * (3 + 4 * part) // 16
     return pl.pallas_call(
-        functools.partial(attend_kernel, pairs, step),
-        out_shape=[jax.ShapeDtypeStruct((rows, c), jnp.bfloat16) for c in shapes],
+        functools.partial(attend_kernel, pairs, step, part),
+        out_shape=[jax.ShapeDtypeStruct(shape, jnp.bfloat16) for shape in shapes],
         compiler_params=params(26, False),
-        cost_estimate=cost(4 * area * LANES, 10 * qkv.size, area),
+        cost_estimate=cost(4 * area * LANES, 10 * inputs[0].size, area),
         name="attend",
-    )(qkv, cosine, sine)
+    )(*inputs)
 
 
 def attend_back_kernel(pairs, step, group, *refs):
-    q, k, v, heads, dheads, cosine, sine = refs[:7]
+    q, k, v, low, high, dheads, cosine, sine = refs[:8]
     out, dk, dv, dq = refs[-4:]
     rows = cosine.shape[0]
     cos, sin = cosine[...], sine[...]
@@ -153,9 +166,9 @@
     width = 2 * pairs * HD
     flat_q = jnp.zeros((rows, width), jnp.float32)
     flat_kv = jnp.zeros((rows, width), jnp.float32)
-    if len(refs) > 11:
-        flat_q += refs[7][:, :width].astype(jnp.float32)
-        flat_kv += refs[7][:, width:].astype(jnp.float32)
+    if len(refs) > 12:
+        flat_q += refs[8][:, :width].astype(jnp.float32)
+        flat_kv += refs[8][:, width:].astype(jnp.float32)
     for g in (group,):
         kv = slice(g * LANES, (g + 1) * LANES)
         dk[...] = jnp.zeros_like(dk)
@@ -166,14 +179,17 @@
             past = slice(start, (block + 1) * step)
             one, two = (slice((2 * g + e) * LANES, (2 * g + e + 1) * LANES) for e in range(2))
 
-            def both(ref):
-                return jnp.concatenate([ref[here, one], ref[here, two]], axis=0)
-
-            query, dhead = both(q), both(dheads)
+            def both(ref, at):
+                return jnp.concatenate([ref[at, one], ref[at, two]], axis=0)
+
+            query, dhead = both(q, here), both(dheads, here)
+            upper = 2 * block * step >= rows
+            first = block * step - (rows // 2 if upper else 0)
+            head = both(high if upper else low, slice(first, first + step))
             prob = softmax_block(query, k[past, kv], block, step, start)
             dv[past] += dot(prob.astype(jnp.bfloat16), dhead, TN)
             delta = jnp.sum(
-                dhead.astype(jnp.float32) * both(heads).astype(jnp.float32), axis=1, keepdims=True
+                dhead.astype(jnp.float32) * head.astype(jnp.float32), axis=1, keepdims=True
             )
             dscore = (prob * (dot(dhead, v[past, kv], NT) - delta)).astype(jnp.bfloat16)
             dk[past] += dot(dscore, query, TN)
@@ -190,7 +206,7 @@
     out[:, width:] = flat_kv.astype(jnp.bfloat16)
 
 
-def attend_back(q, k, v, heads, dheads, cosine, sine, pairs, step, group, before):
+def attend_back(q, k, v, low, high, dheads, cosine, sine, pairs, step, group, before):
     rows = q.shape[0]
     area = rows * min(rows, L) * 2 * 5 // 8
     held = [] if before is None else [before]
@@ -205,7 +221,7 @@
         compiler_params=params(26, False),
         cost_estimate=cost(10 * area * LANES, 10 * q.size, area),
         name="attend_back",
-    )(q, k, v, heads, dheads, cosine, sine, *held)
+    )(q, k, v, low, high, dheads, cosine, sine, *held)
 
 
 def place_kernel(count, me, *refs):
@@ -264,44 +280,65 @@
     )(me, gain[None, :], *blocks)
 
 
-def project_kernel(count, me, inputs, gain, *refs):
-    attended, weight, normed, own = refs[:count], *refs[count:]
-    joined = jnp.concatenate([a[...] for a in attended], axis=1)
-    value = inputs[...].astype(jnp.float32) + dot(joined, weight[...], NN)
+def project_kernel(count, kinds, part, info, inputs, gain, *refs):
+    attended, weights = refs[:count], refs[count : count + len(kinds)]
+    normed, own, joined = refs[-3:]
+    here = pl.program_id(0)
+
+    @pl.when(here == 0)
+    def _():
+        for weight, (base, kind) in zip(weights, kinds):
+            depth = weight.shape[0]
+            if kind:
+                shift = info[1] if kind == 1 else 1 - info[1]
+                base = pl.multiple_of(base + shift * depth, 16)
+            joined[pl.ds(base, depth)] = weight[...]
+        if part:
+            own[...] = refs[count + len(kinds) + 1][...]
+
+    features = jnp.concatenate([a[...] for a in attended], axis=1)
+    value = inputs[...].astype(jnp.float32) + dot(features, joined[...], NN)
     recip = lax.rsqrt(jnp.mean(value * value, axis=-1, keepdims=True) + EPS)
     normed[...] = (value * recip * gain[...]).astype(jnp.bfloat16)
 
-    @pl.when(pl.program_id(0) == me[0])
+    @pl.when(here + part * pl.num_programs(0) == info[0])
     def _():
         own[...] = value
 
 
-def project(inputs, gain, attended, weight, me):
+def project(inputs, gain, attended, weights, info, part, before):
     count = len(attended)
     rows_all, columns = inputs.shape
-    rows = rows_all // count
+    rows, steps = rows_all // count, count // 2
     depth = attended[0].shape[1]
-    mine = pl.BlockSpec((rows, columns), lambda s, m: (s, 0))
+    mine = pl.BlockSpec((rows, columns), lambda s, m: (s + part * steps, 0))
+    own = pl.BlockSpec((rows, columns), lambda s, m: (0, 0))
+    held = [] if before is None else list(before)
+    kinds = [kind for _, kind in weights]
+    place_of = 3 + count + len(weights)
     return pl.pallas_call(
-        functools.partial(project_kernel, count),
+        functools.partial(project_kernel, count, kinds, part),
         out_shape=[
             jax.ShapeDtypeStruct((rows_all, columns), jnp.bfloat16),
             jax.ShapeDtypeStruct((rows, columns), jnp.float32),
         ],
         grid_spec=pltpu.PrefetchScalarGridSpec(
             num_scalar_prefetch=1,
-            grid=(count,),
+            grid=(steps,),
             in_specs=[mine, whole((1, columns))]
             + [pl.BlockSpec((rows, depth), lambda s, m: (s, 0))] * count
-            + [whole(weight.shape)],
-            out_specs=[mine, pl.BlockSpec((rows, columns), lambda s, m: (0, 0))],
+            + [whole(weight.shape) for weight, _ in weights]
+            + ([pl.BlockSpec(memory_space=pl.ANY), whole((rows, columns))] if held else []),
+            out_specs=[mine, own],
+            scratch_shapes=[pltpu.VMEM((count * depth, columns), jnp.bfloat16)],
         ),
-        compiler_params=params(30),
+        input_output_aliases={place_of: 0} if held else {},
+        compiler_params=params(40),
         cost_estimate=cost(
-            2 * rows_all * depth * count * columns, 6 * inputs.size + 2 * weight.size
+            rows_all * depth * count * columns, 3 * inputs.size + 2 * count * depth * columns
         ),
         name="project",
-    )(me, inputs, gain[None, :], *attended, weight)
+    )(info, inputs, gain[None, :], *attended, *[weight for weight, _ in weights], *held)
 
 
 def swap(value, axis, size, bit):
@@ -317,21 +354,21 @@
 
 
 def gather_weight(weight, size, dp):
-    far = size // 2
-    blocks = {0: weight}
+    far, rows = size // 2, weight.shape[0]
+    blocks = {0: [(weight, 0)]}
     if dp % 2 == 0 and size >= 4:
-        half = weight.shape[0] // 2
+        half = rows // 2
         side = lax.axis_index("dp") & 1
         part = lax.dynamic_slice(weight, (side * half, 0), (half, weight.shape[1]))
         part = swap(part, "tensor", size, far)
-        other = swap(part, "dp", dp, 1)
-        first, second = jnp.where(side == 0, part, other), jnp.where(side == 0, other, part)
-        blocks[far] = jnp.concatenate([first, second], axis=0)
+        blocks[far] = [(part, 1), (swap(part, "dp", dp, 1), 2)]
     for j in range(1, size):
         if j not in blocks:
             low = j & -j
-            blocks[j] = swap(blocks[j ^ low], "tensor", size, low)
-    return jnp.concatenate([blocks[j] for j in range(size)], axis=0)
+            blocks[j] = [
+                (swap(piece, "tensor", size, low), kind) for piece, kind in blocks[j ^ low]
+            ]
+    return [(piece, (j * rows, kind)) for j in range(size) for piece, kind in blocks[j]]
 
 
 def scatter_sum(array, size, me):
@@ -540,11 +577,17 @@
 
         blocks = gather_blocks(block_input, tensor)
         full_one, full_inputs = norm_place(blocks, gain_attention, spot)
-        weight = gather_weight(after(w_output, blocks[-1]), tensor, dp)
+        weights = gather_weight(after(w_output, blocks[-1]), tensor, dp)
         qkv = dot(full_one, w_padded, NN)
-        heads, flat, q, k, v = attend(qkv, cosine, sine, pairs, step)
-        attended = gather_blocks(flat, tensor)
-        full_two, resid = project(full_inputs, gain_feedforward, attended, weight, spot)
+        low, flat_low, q, k, v = attend((qkv, cosine, sine), pairs, step, 0)
+        high, flat_high = attend((q, k, v), pairs, step, 1)
+        heads = (low, high)
+        attended_low = gather_blocks(flat_low, tensor)
+        attended = gather_blocks(flat_high, tensor)
+        info = jnp.stack([me, lax.axis_index("dp") & 1]).astype(jnp.int32)
+        halves = project(full_inputs, gain_feedforward, attended_low, weights, info, 0, None)
+        full_two, resid = project(full_inputs, gain_feedforward, attended, weights, info, 1, halves)
+        flat = jnp.concatenate([flat_low, flat_high], axis=0)
         full_grad = place(gather_blocks(after(cotangent, attended[-1]), tensor), spot)
 
         gate = dot(full_two, w_gate, NN)
@@ -576,7 +619,7 @@
         dqkv = None
         for group in range(pairs):
             dqkv = attend_back(
-                q, k, v, heads, dheads, cosine, sine, pairs, step, group, dqkv
+                q, k, v, *heads, dheads, cosine, sine, pairs, step, group, dqkv
             )
         grad_output = dot(flat, full_dresid, TN).astype(jnp.bfloat16)
         dquery, dboth = dqkv[:, : 2 * pair_cols], dqkv[:, 2 * pair_cols :]

time: 502 us -> 517 us (1.030)
  local copies, waits for them, and re-layouts: 25.2 us -> 35.8 us
  matrix products: 62.5 us -> 53.2 us
  Pallas kernels: 75.2 us -> 81.6 us
    ppermute x56, starting transfers between devices: 54.2 us -> 64.5 us  [hop(): return lax.ppermute(value, 'dp', hops[(1, -1)[k]])]
    ppermute x30 -> x34, waiting for transfers between devices: 69 us -> 78.7 us  [swap(): return lax.ppermute(value, axis, [(i, i ^ bit) for i in range(size)])]
    unnamed x139 -> x161, local copies, waits for them, and re-layouts: 9.34 us -> 18.8 us
    dot_general x16, matrix products: 62.5 us -> 53.2 us  [dot(): lax.dot_general(left, right, (dims, ((), ())), preferred_element_type=jnp...]
    ppermute x30 -> x34, starting transfers between devices: 25.1 us -> 18.8 us  [swap(): return lax.ppermute(value, axis, [(i, i ^ bit) for i in range(size)])]
    pallas_call x2 -> x4, Pallas kernels: 17.3 us -> 21.3 us  [the longest x2 13.8 us: project(): pl.pallas_call(functools.partial(project_kernel, count, kinds, part), out...]
  transfers between devices with their start and end apart: 86 -> 90, of which waited for: 43 -> 42; matrix products, arithmetic and copies ran while one was open for 15% -> 12% of each run, Pallas kernels for 14% -> 14%
where the time goes in v1:
time: 517 us; the launch traced here: 512 us
  waiting for transfers between devices  239 us (46%)
  starting transfers between devices  83.4 us (16%)
  Pallas kernels  81.6 us (16%)
  matrix products  53.2 us (10%)
  local copies, waits for them, and re-layouts  35.8 us (7%)
  other arithmetic  16.9 us (3%)
    ppermute x56, waiting for transfers between devices, hop(): return lax.ppermute(value, 'dp', hops[(1, -1)[k]])  160 us
    ppermute x34, waiting for transfers between devices, swap(): return lax.ppermute(value, axis, [(i, i ^ bit) for i in range(size)])  78.7 us
    ppermute x56, starting transfers between devices, hop(): return lax.ppermute(value, 'dp', hops[(1, -1)[k]])  64.5 us
    dot_general x16, matrix products, dot(): lax.dot_general(left, right, (dims, ((), ())), preferred_element_type=jnp...  53.2 us
    pallas_call x8, Pallas kernels, unpack(): pl.pallas_call(functools.partial(unpack_kernel, [span[0] for span in span...  35.9 us
    ppermute x34, starting transfers between devices, swap(): return lax.ppermute(value, axis, [(i, i ^ bit) for i in range(size)])  18.8 us
    unnamed x161, local copies, waits for them, and re-layouts  18.8 us
    pallas_call x2, Pallas kernels, project(): pl.pallas_call(functools.partial(project_kernel, count, kinds, part), out...  13.8 us
  transfers between devices with their start and end apart: 90, of which 42 were waited for; matrix products, arithmetic and copies ran while one was open for 12% of the time, Pallas kernels for 14%

profile of v1, /device:TPU:0, one launch (start us, length us, event | category | flops | bytes accessed | tf_op | source)
XLA Modules:
  0.0 511.7 jit_solution(12088388452909765065)
XLA Ops:
  3.7 17.9 %collective-permute-done.1.refs_2_ = bf16[256,1536]{1,0:T(8,128)(2,1)} collective-permute-done((bf16[256,1536]{1,0:T(8,128)(2,1)}, bf16[256,1536]{1,0:T(8,128)(2,1)}, u32[]{:S(2)}, u32[]{:S(2)}) %collective-permute-start.1) | collective-permute-done | bytes 786464 | tf_op jit(solution)/shard_map/ppermute | solution.py:345
  55.9 10.5 %collective-permute-done.4.refs_2_ = bf16[512,384]{1,0:T(8,128)(2,1)S(1)} collective-permute-done((bf16[512,384]{1,0:T(8,128)(2,1)S(1)}, bf16[512,384]{1,0:T(8,128)(2,1)S(1)}, u32[]{:S(2)}, u32[]{:S(2)}) %collective-permute-start.4) | collective-permute-done | bytes 393248 | tf_op jit(solution)/shard_map/ppermute | solution.py:345
  71.8 9.2 %collective-permute-done.12.refs_2_ = bf16[512,384]{1,0:T(8,128)(2,1)S(1)} collective-permute-done((bf16[512,384]{1,0:T(8,128)(2,1)S(1)}, bf16[512,384]{1,0:T(8,128)(2,1)S(1)}, u32[]{:S(2)}, u32[]{:S(2)}) %collective-permute-start.12) | collective-permute-done | bytes 393248 | tf_op jit(solution)/shard_map/ppermute | solution.py:345
  87.3 9.5 %collective-permute-done.15.refs_2_ = bf16[256,1536]{1,0:T(8,128)(2,1)} collective-permute-done((bf16[256,1536]{1,0:T(8,128)(2,1)}, bf16[256,1536]{1,0:T(8,128)(2,1)}, u32[]{:S(2)}, u32[]{:S(2)}) %collective-permute-start.15) | collective-permute-done | bytes 786464 | tf_op jit(solution)/shard_map/ppermute | solution.py:345
  102.7 6.5 %project.2 = (bf16[1024,1536]{1,0:T(8,128)(2,1)S(1)}, f32[256,1536]{1,0:T(8,128)S(1)}) custom-call(s32[2]{0:T(128)S(1)} %pad_add_fusion.info, bf16[1024,1536]{1,0:T(8,128)(2,1)S(1)} %copy-done.3, f32[1,1536]{1,0:T(1,128)S(1)} %broadcast_in_dim.5.gain, bf16[512,384]{1,0:T(8,128)(2,1)S(1)} %copy-done.25, bf16[512,384]{1,0:T(8,128)(2,1)S(1)} %copy-done.30, ...), custom_call_target="tpu_custom_call" | custom-call | flops 2415919104 | bytes 9437184 | tf_op jit(solution)/shard_map/project/pallas_call | solution.py:319
  109.3 7.2 %project.3 = (bf16[1024,1536]{1,0:T(8,128)(2,1)S(1)}, f32[256,1536]{1,0:T(8,128)S(1)}) custom-call(s32[2]{0:T(128)S(1)} %pad_add_fusion.info, bf16[1024,1536]{1,0:T(8,128)(2,1)} %copy-done.2, f32[1,1536]{1,0:T(1,128)S(1)} %broadcast_in_dim.5.gain, bf16[512,384]{1,0:T(8,128)(2,1)S(1)} %get-tuple-element.58.refs_0_, ...), custom_call_target="tpu_custom_call", output_to_operand_aliasing={{0}: (13, {})} | custom-call | flops 2415919104 | bytes 9437184 | tf_op jit(solution)/shard_map/project/pallas_call | solution.py:319
  125.9 6.6 %multiply_convert_fusion = (bf16[1024,1024]{1,0:T(8,128)(2,1)}, bf16[1024,1024]{1,0:T(8,128)(2,1)S(1)}, bf16[1024,1024]{1,0:T(8,128)(2,1)S(1)}) fusion(f32[1024,1024]{1,0:T(8,128)S(1)} %fusion.38, f32[1024,1024]{1,0:T(8,128)S(1)} %fusion.37, bf16[1024,1536]{1,0:T(8,128)(2,1)S(1)} %get-tuple-element.64, bf16[1536,1024]{1,0:T(8,128)(2,1)S(1)} %copy-done), kind=kOutput, calls=%fused_computation.2 | convolution fusion | flops 3236954112 | bytes 20971520 | tf_op jit(solution)/shard_map/dot_general | solution.py:62
  160.8 7.3 %collective-permute-done.76 = bf16[1152,256]{1,0:T(8,128)(2,1)S(1)} collective-permute-done((bf16[1152,256]{1,0:T(8,128)(2,1)S(1)}, bf16[1152,256]{1,0:T(8,128)(2,1)S(1)}, u32[]{:S(2)}, u32[]{:S(2)}) %collective-permute-start.76) | collective-permute-done | bytes 589856 | tf_op jit(solution)/shard_map/ppermute | solution.py:507
  171.4 11.8 %collective-permute-done.77 = bf16[1152,256]{1,0:T(8,128)(2,1)S(1)} collective-permute-done((bf16[1152,256]{1,0:T(8,128)(2,1)S(1)}, bf16[1152,256]{1,0:T(8,128)(2,1)S(1)}, u32[]{:S(2)}, u32[]{:S(2)}) %collective-permute-start.77) | collective-permute-done | bytes 589856 | tf_op jit(solution)/shard_map/ppermute | solution.py:507
  190.2 7.3 %collective-permute-done.78 = bf16[1152,256]{1,0:T(8,128)(2,1)S(1)} collective-permute-done((bf16[1152,256]{1,0:T(8,128)(2,1)S(1)}, bf16[1152,256]{1,0:T(8,128)(2,1)S(1)}, u32[]{:S(2)}, u32[]{:S(2)}) %collective-permute-start.78) | collective-permute-done | bytes 589856 | tf_op jit(solution)/shard_map/ppermute | solution.py:507
  202.5 8.5 %collective-permute-done.79 = bf16[1152,256]{1,0:T(8,128)(2,1)S(1)} collective-permute-done((bf16[1152,256]{1,0:T(8,128)(2,1)S(1)}, bf16[1152,256]{1,0:T(8,128)(2,1)S(1)}, u32[]{:S(2)}, u32[]{:S(2)}) %collective-permute-start.79) | collective-permute-done | bytes 589856 | tf_op jit(solution)/shard_map/ppermute | solution.py:507
  231.8 6.5 %attend_back.2.refs_8_ = bf16[1024,768]{1,0:T(8,128)(2,1)S(1)} custom-call(bf16[1024,512]{1,0:T(8,128)(2,1)S(1)} %copy-done.11, bf16[1024,256]{1,0:T(8,128)(2,1)S(1)} %copy-done.15, bf16[1024,256]{1,0:T(8,128)(2,1)S(1)} %copy-done.17, bf16[512,512]{1,0:T(8,128)(2,1)S(1)} %copy-done.13, bf16[512,512]{1,0:T(8,128)(2,1)S(1)} %copy-done.19, ...), custom_call_target="tpu_custom_call" | custom-call | flops 1677721600 | bytes 5242880 | tf_op jit(solution)/shard_map/attend_back/pallas_call | solution.py:213
  238.3 6.7 %attend_back.3 = bf16[1024,768]{1,0:T(8,128)(2,1)S(1)} custom-call(bf16[1024,512]{1,0:T(8,128)(2,1)S(1)} %copy-done.11, bf16[1024,256]{1,0:T(8,128)(2,1)S(1)} %copy-done.15, bf16[1024,256]{1,0:T(8,128)(2,1)S(1)} %copy-done.17, bf16[512,512]{1,0:T(8,128)(2,1)S(1)} %copy-done.13, bf16[512,512]{1,0:T(8,128)(2,1)S(1)} %copy-done.19, ...), custom_call_target="tpu_custom_call" | custom-call | flops 1677721600 | bytes 5242880 | tf_op jit(solution)/shard_map/attend_back/pallas_call | solution.py:213
  293.6 12.9 %collective-permute-done.51 = bf16[288,384]{1,0:T(8,128)(2,1)S(1)} collective-permute-done((bf16[288,384]{1,0:T(8,128)(2,1)S(1)}, bf16[288,384]{1,0:T(8,128)(2,1)S(1)}, u32[]{:S(2)}, u32[]{:S(2)}) %collective-permute-start.51) | collective-permute-done | bytes 221216 | tf_op jit(solution)/shard_map/ppermute | solution.py:507
  308.2 6.5 %collective-permute-done.37 = bf16[288,384]{1,0:T(8,128)(2,1)S(1)} collective-permute-done((bf16[288,384]{1,0:T(8,128)(2,1)S(1)}, bf16[288,384]{1,0:T(8,128)(2,1)S(1)}, u32[]{:S(2)}, u32[]{:S(2)}) %collective-permute-start.37) | collective-permute-done | bytes 221216 | tf_op jit(solution)/shard_map/ppermute | solution.py:507
  317.3 7.3 %collective-permute-done.68 = bf16[1152,256]{1,0:T(8,128)(2,1)S(1)} collective-permute-done((bf16[1152,256]{1,0:T(8,128)(2,1)S(1)}, bf16[1152,256]{1,0:T(8,128)(2,1)S(1)}, u32[]{:S(2)}, u32[]{:S(2)}) %collective-permute-start.68) | collective-permute-done | bytes 589856 | tf_op jit(solution)/shard_map/ppermute | solution.py:507
  338.2 6.0 %collective-permute-done.53 = bf16[288,384]{1,0:T(8,128)(2,1)S(1)} collective-permute-done((bf16[288,384]{1,0:T(8,128)(2,1)S(1)}, bf16[288,384]{1,0:T(8,128)(2,1)S(1)}, u32[]{:S(2)}, u32[]{:S(2)}) %collective-permute-start.53) | collective-permute-done | bytes 221216 | tf_op jit(solution)/shard_map/ppermute | solution.py:507
  349.0 8.8 %collective-permute-done.39 = bf16[288,384]{1,0:T(8,128)(2,1)S(1)} collective-permute-done((bf16[288,384]{1,0:T(8,128)(2,1)S(1)}, bf16[288,384]{1,0:T(8,128)(2,1)S(1)}, u32[]{:S(2)}, u32[]{:S(2)}) %collective-permute-start.39) | collective-permute-done | bytes 221216 | tf_op jit(solution)/shard_map/ppermute | solution.py:507
  370.7 7.6 %collective-permute-done.84.refs_6_ = bf16[1152,256]{1,0:T(8,128)(2,1)S(1)} collective-permute-done((bf16[1152,256]{1,0:T(8,128)(2,1)S(1)}, bf16[1152,256]{1,0:T(8,128)(2,1)S(1)}, u32[]{:S(2)}, u32[]{:S(2)}) %collective-permute-start.84) | collective-permute-done | bytes 589856 | tf_op jit(solution)/shard_map/ppermute | solution.py:507
  383.1 11.8 %collective-permute-done.31 = f32[2,1536]{1,0:T(2,128)S(1)} collective-permute-done((f32[2,1536]{1,0:T(2,128)S(1)}, f32[2,1536]{1,0:T(2,128)S(1)}, u32[]{:S(2)}, u32[]{:S(2)}) %collective-permute-start.31) | collective-permute-done | bytes 12320 | tf_op jit(solution)/shard_map/ppermute | solution.py:345
  403.2 12.2 %collective-permute-done.56.refs_6_ = bf16[288,384]{1,0:T(8,128)(2,1)S(1)} collective-permute-done((bf16[288,384]{1,0:T(8,128)(2,1)S(1)}, bf16[288,384]{1,0:T(8,128)(2,1)S(1)}, u32[]{:S(2)}, u32[]{:S(2)}) %collective-permute-start.56) | collective-permute-done | bytes 221216 | tf_op jit(solution)/shard_map/ppermute | solution.py:507
  432.9 11.7 %collective-permute-done.59.refs_3_ = bf16[288,384]{1,0:T(8,128)(2,1)S(1)} collective-permute-done((bf16[288,384]{1,0:T(8,128)(2,1)S(1)}, bf16[288,384]{1,0:T(8,128)(2,1)S(1)}, u32[]{:S(2)}, u32[]{:S(2)}) %collective-permute-start.59) | collective-permute-done | bytes 221216 | tf_op jit(solution)/shard_map/ppermute | solution.py:507
  457.1 9.1 %collective-permute-done.33 = f32[2,1536]{1,0:T(2,128)S(1)} collective-permute-done((f32[2,1536]{1,0:T(2,128)S(1)}, f32[2,1536]{1,0:T(2,128)S(1)}, u32[]{:S(2)}, u32[]{:S(2)}) %collective-permute-start.33) | collective-permute-done | bytes 12320 | tf_op jit(solution)/shard_map/ppermute | solution.py:345
  480.3 8.1 %unpack.12 = (f32[1536,1024]{1,0:T(8,128)}, f32[1536,1024]{1,0:T(8,128)}, f32[1024,1536]{1,0:T(8,128)}) custom-call(s32[1]{0:T(128)} %dynamic_slice.58.start, bf16[1152,256]{1,0:T(8,128)(2,1)} %copy-done.39, bf16[1152,256]{1,0:T(8,128)(2,1)} %copy-done.46, bf16[1152,256]{1,0:T(8,128)(2,1)} %copy-done.48, bf16[1152,256]{1,0:T(8,128)(2,1)} %copy-done.50, ...), custom_call_target="tpu_custom_call" | custom-call | bytes 14155776 | tf_op jit(solution)/shard_map/unpack/pallas_call | solution.py:472
  (428 shorter events, 292.2 us)
Async XLA Ops:
  35.7 31.9 %collective-permute-start.7 = (bf16[192,1536]{1,0:T(8,128)(2,1)S(1)}, bf16[192,1536]{1,0:T(8,128)(2,1)}, u32[]{:S(2)}, u32[]{:S(2)}) collective-permute-start(bf16[192,1536]{1,0:T(8,128)(2,1)S(1)} %constant_dynamic-slice_fusion.6), channel_id=1, source_target_pairs={{0,2},{1,3},{2,0},{3,1},{4,6},{5,7},{6,4},{7,5},{8,10},{9,11},{10,... | collective-permute-start | bytes 1769480 | tf_op jit(solution)/shard_map/ppermute | solution.py:345
  67.1 29.7 %collective-permute-start.6 = (bf16[384,1536]{1,0:T(8,128)(2,1)}, bf16[384,1536]{1,0:T(8,128)(2,1)}, u32[]{:S(2)}, u32[]{:S(2)}) collective-permute-start(bf16[384,1536]{1,0:T(8,128)(2,1)} %refs_4_.1), channel_id=1, source_target_pairs={{0,1},{1,0},{2,3},{3,2},{4,5},{5,4},{6,7},{7,6},{8,9},{9,8},{10,11... | collective-permute-start | bytes 3538952 | tf_op jit(solution)/shard_map/ppermute | solution.py:345
  70.3 26.4 %collective-permute-start.15 = (bf16[256,1536]{1,0:T(8,128)(2,1)}, bf16[256,1536]{1,0:T(8,128)(2,1)}, u32[]{:S(2)}, u32[]{:S(2)}) collective-permute-start(bf16[256,1536]{1,0:T(8,128)(2,1)} %refs_0_.2), channel_id=1, source_target_pairs={{0,2},{1,3},{2,0},{3,1},{4,6},{5,7},{6,4},{7,5},{8,10},{9,11},{10,... | collective-permute-start | bytes 2359304 | tf_op jit(solution)/shard_map/ppermute | solution.py:345
  83.9 25.3 %collective-permute-start.3 = (bf16[512,384]{1,0:T(8,128)(2,1)S(1)}, bf16[512,384]{1,0:T(8,128)(2,1)}, u32[]{:S(2)}, u32[]{:S(2)}) collective-permute-start(bf16[512,384]{1,0:T(8,128)(2,1)S(1)} %get-tuple-element.58.refs_0_), channel_id=1, source_target_pairs={{0,1},{1,0},{2,3},{3,2},{4,5},{5,4},{6,7},{7,6},{8,9},{9,8},{10,11... | collective-permute-start | bytes 1179656 | tf_op jit(solution)/shard_map/ppermute | solution.py:345
  87.2 32.9 %collective-permute-start.14 = (bf16[256,1536]{1,0:T(8,128)(2,1)}, bf16[256,1536]{1,0:T(8,128)(2,1)S(1)}, u32[]{:S(2)}, u32[]{:S(2)}) collective-permute-start(bf16[256,1536]{1,0:T(8,128)(2,1)} %refs_0_.2), channel_id=1, source_target_pairs={{0,1},{1,0},{2,3},{3,2},{4,5},{5,4},{6,7},{7,6},{8,9},{9,8},{10,11... | collective-permute-start | bytes 2359304 | tf_op jit(solution)/shard_map/ppermute | solution.py:345
  96.8 23.4 %collective-permute-start.16 = (bf16[256,1536]{1,0:T(8,128)(2,1)}, bf16[256,1536]{1,0:T(8,128)(2,1)S(1)}, u32[]{:S(2)}, u32[]{:S(2)}) collective-permute-start(bf16[256,1536]{1,0:T(8,128)(2,1)} %collective-permute-done.15.refs_2_), channel_id=1, source_target_pairs={{0,1},{1,0},{2,3},{3,2},{4,5},{5,4},{6,7},{7,6},{8,9},{9,8},{10,11... | collective-permute-start | bytes 2359304 | tf_op jit(solution)/shard_map/ppermute | solution.py:345
  160.2 25.5 %collective-permute-start.17 = (bf16[256,1536]{1,0:T(8,128)(2,1)S(1)}, bf16[256,1536]{1,0:T(8,128)(2,1)S(1)}, u32[]{:S(2)}, u32[]{:S(2)}) collective-permute-start(bf16[256,1536]{1,0:T(8,128)(2,1)S(1)} %get-tuple-element.110), channel_id=1, source_target_pairs={{0,1},{1,0},{2,3},{3,2},{4,5},{5,4},{6,7},{7,6},{8,9},{9,8},{10,11... | collective-permute-start | bytes 2359304 | tf_op jit(solution)/shard_map/ppermute | solution.py:345
  224.5 39.1 %collective-permute-start.81 = (bf16[1152,256]{1,0:T(8,128)(2,1)}, bf16[1152,256]{1,0:T(8,128)(2,1)S(1)}, u32[]{:S(2)}, u32[]{:S(2)}) collective-permute-start(bf16[1152,256]{1,0:T(8,128)(2,1)} %add_convert_fusion.8), channel_id=1, source_target_pairs={{0,4},{8,0},{16,8},{24,16},{28,24},{20,28},{12,20},{4,12},{1,5},{9... | collective-permute-start | bytes 1769480 | tf_op jit(solution)/shard_map/ppermute | solution.py:507
  225.9 38.3 %collective-permute-start.67 = (bf16[1152,256]{1,0:T(8,128)(2,1)}, bf16[1152,256]{1,0:T(8,128)(2,1)}, u32[]{:S(2)}, u32[]{:S(2)}) collective-permute-start(bf16[1152,256]{1,0:T(8,128)(2,1)} %add_convert_fusion.15), channel_id=1, source_target_pairs={{0,8},{8,16},{16,24},{24,28},{28,20},{20,12},{12,4},{4,0},{1,9},{9... | collective-permute-start | bytes 1769480 | tf_op jit(solution)/shard_map/ppermute | solution.py:507
  260.2 122.3 %collective-permute-start.23 = (bf16[256,1536]{1,0:T(8,128)(2,1)}, bf16[256,1536]{1,0:T(8,128)(2,1)S(1)}, u32[]{:S(2)}, u32[]{:S(2)}) collective-permute-start(bf16[256,1536]{1,0:T(8,128)(2,1)} %get-tuple-element.108), channel_id=1, source_target_pairs={{0,1},{1,0},{2,3},{3,2},{4,5},{5,4},{6,7},{7,6},{8,9},{9,8},{10,11... | collective-permute-start | bytes 2359304 | tf_op jit(solution)/shard_map/ppermute | solution.py:345
  262.9 155.5 %collective-permute-start.24 = (bf16[256,1536]{1,0:T(8,128)(2,1)}, bf16[256,1536]{1,0:T(8,128)(2,1)S(1)}, u32[]{:S(2)}, u32[]{:S(2)}) collective-permute-start(bf16[256,1536]{1,0:T(8,128)(2,1)} %get-tuple-element.109), channel_id=1, source_target_pairs={{0,1},{1,0},{2,3},{3,2},{4,5},{5,4},{6,7},{7,6},{8,9},{9,8},{10,11... | collective-permute-start | bytes 2359304 | tf_op jit(solution)/shard_map/ppermute | solution.py:345
  263.4 82.0 %collective-permute-start.26 = (bf16[256,1536]{1,0:T(8,128)(2,1)S(1)}, bf16[256,1536]{1,0:T(8,128)(2,1)S(1)}, u32[]{:S(2)}, u32[]{:S(2)}) collective-permute-start(bf16[256,1536]{1,0:T(8,128)(2,1)S(1)} %get-tuple-element.106), channel_id=1, source_target_pairs={{0,1},{1,0},{2,3},{3,2},{4,5},{5,4},{6,7},{7,6},{8,9},{9,8},{10,11... | collective-permute-start | bytes 2359304 | tf_op jit(solution)/shard_map/ppermute | solution.py:345
  263.6 28.0 %collective-permute-start.27 = (bf16[256,1536]{1,0:T(8,128)(2,1)S(1)}, bf16[256,1536]{1,0:T(8,128)(2,1)S(1)}, u32[]{:S(2)}, u32[]{:S(2)}) collective-permute-start(bf16[256,1536]{1,0:T(8,128)(2,1)S(1)} %get-tuple-element.107), channel_id=1, source_target_pairs={{0,1},{1,0},{2,3},{3,2},{4,5},{5,4},{6,7},{7,6},{8,9},{9,8},{10,11... | collective-permute-start | bytes 2359304 | tf_op jit(solution)/shard_map/ppermute | solution.py:345
  290.3 26.2 %collective-permute-start.82 = (bf16[1152,256]{1,0:T(8,128)(2,1)S(1)}, bf16[1152,256]{1,0:T(8,128)(2,1)S(1)}, u32[]{:S(2)}, u32[]{:S(2)}) collective-permute-start(bf16[1152,256]{1,0:T(8,128)(2,1)S(1)} %add_convert_fusion.7), channel_id=1, source_target_pairs={{0,4},{8,0},{16,8},{24,16},{28,24},{20,28},{12,20},{4,12},{1,5},{9... | collective-permute-start | bytes 1769480 | tf_op jit(solution)/shard_map/ppermute | solution.py:507
  316.5 29.8 %collective-permute-start.28 = (bf16[256,1536]{1,0:T(8,128)(2,1)S(1)}, bf16[256,1536]{1,0:T(8,128)(2,1)S(1)}, u32[]{:S(2)}, u32[]{:S(2)}) collective-permute-start(bf16[256,1536]{1,0:T(8,128)(2,1)S(1)} %add_convert_fusion.2), channel_id=1, source_target_pairs={{0,2},{1,3},{2,0},{3,1},{4,6},{5,7},{6,4},{7,5},{8,10},{9,11},{10,... | collective-permute-start | bytes 2359304 | tf_op jit(solution)/shard_map/ppermute | solution.py:345
  394.9 29.8 %collective-permute-start.86 = (bf16[1152,256]{1,0:T(8,128)(2,1)S(1)}, bf16[1152,256]{1,0:T(8,128)(2,1)S(1)}, u32[]{:S(2)}, u32[]{:S(2)}) collective-permute-start(bf16[1152,256]{1,0:T(8,128)(2,1)S(1)} %collective-permute-done.85.refs_7_), channel_id=1, source_target_pairs={{0,4},{8,0},{16,8},{24,16},{28,24},{20,28},{12,20},{4,12},{1,5},{9... | collective-permute-start | bytes 1769480 | tf_op jit(solution)/shard_map/ppermute | solution.py:507
  396.9 29.5 %collective-permute-start.72 = (bf16[1152,256]{1,0:T(8,128)(2,1)S(1)}, bf16[1152,256]{1,0:T(8,128)(2,1)S(1)}, u32[]{:S(2)}, u32[]{:S(2)}) collective-permute-start(bf16[1152,256]{1,0:T(8,128)(2,1)S(1)} %collective-permute-done.71.refs_3_), channel_id=1, source_target_pairs={{0,8},{8,16},{16,24},{24,28},{28,20},{20,12},{12,4},{4,0},{1,9},{9... | collective-permute-start | bytes 1769480 | tf_op jit(solution)/shard_map/ppermute | solution.py:507
  424.6 22.8 %collective-permute-start.87 = (bf16[1152,256]{1,0:T(8,128)(2,1)S(1)}, bf16[1152,256]{1,0:T(8,128)(2,1)S(1)}, u32[]{:S(2)}, u32[]{:S(2)}) collective-permute-start(bf16[1152,256]{1,0:T(8,128)(2,1)S(1)} %collective-permute-done.86.refs_2_), channel_id=1, source_target_pairs={{0,4},{8,0},{16,8},{24,16},{28,24},{20,28},{12,20},{4,12},{1,5},{9... | collective-permute-start | bytes 1769480 | tf_op jit(solution)/shard_map/ppermute | solution.py:507
  426.5 22.4 %collective-permute-start.73 = (bf16[1152,256]{1,0:T(8,128)(2,1)S(1)}, bf16[1152,256]{1,0:T(8,128)(2,1)S(1)}, u32[]{:S(2)}, u32[]{:S(2)}) collective-permute-start(bf16[1152,256]{1,0:T(8,128)(2,1)S(1)} %collective-permute-done.72.refs_0_), channel_id=1, source_target_pairs={{0,8},{8,16},{16,24},{24,28},{28,20},{20,12},{12,4},{4,0},{1,9},{9... | collective-permute-start | bytes 1769480 | tf_op jit(solution)/shard_map/ppermute | solution.py:507
  427.0 24.3 %collective-permute-start.25 = (bf16[256,1536]{1,0:T(8,128)(2,1)S(1)}, bf16[256,1536]{1,0:T(8,128)(2,1)S(1)}, u32[]{:S(2)}, u32[]{:S(2)}) collective-permute-start(bf16[256,1536]{1,0:T(8,128)(2,1)S(1)} %add_convert_fusion.4), channel_id=1, source_target_pairs={{0,2},{1,3},{2,0},{3,1},{4,6},{5,7},{6,4},{7,5},{8,10},{9,11},{10,... | collective-permute-start | bytes 2359304 | tf_op jit(solution)/shard_map/ppermute | solution.py:345
  453.6 37.7 %collective-permute-start.61 = (bf16[288,384]{1,0:T(8,128)(2,1)}, bf16[288,384]{1,0:T(8,128)(2,1)S(1)}, u32[]{:S(2)}, u32[]{:S(2)}) collective-permute-start(bf16[288,384]{1,0:T(8,128)(2,1)} %collective-permute-done.60.refs_1_), channel_id=1, source_target_pairs={{0,4},{8,0},{16,8},{24,16},{28,24},{20,28},{12,20},{4,12},{1,5},{9... | collective-permute-start | bytes 663560 | tf_op jit(solution)/shard_map/ppermute | solution.py:507
  455.3 36.0 %collective-permute-start.47 = (bf16[288,384]{1,0:T(8,128)(2,1)}, bf16[288,384]{1,0:T(8,128)(2,1)S(1)}, u32[]{:S(2)}, u32[]{:S(2)}) collective-permute-start(bf16[288,384]{1,0:T(8,128)(2,1)} %collective-permute-done.46.refs_0_), channel_id=1, source_target_pairs={{0,8},{8,16},{16,24},{24,28},{28,20},{20,12},{12,4},{4,0},{1,9},{9... | collective-permute-start | bytes 663560 | tf_op jit(solution)/shard_map/ppermute | solution.py:507
  466.1 40.6 %collective-permute-start.89 = (bf16[1152,256]{1,0:T(8,128)(2,1)}, bf16[1152,256]{1,0:T(8,128)(2,1)S(1)}, u32[]{:S(2)}, u32[]{:S(2)}) collective-permute-start(bf16[1152,256]{1,0:T(8,128)(2,1)} %collective-permute-done.88.refs_1_), channel_id=1, source_target_pairs={{0,4},{8,0},{16,8},{24,16},{28,24},{20,28},{12,20},{4,12},{1,5},{9... | collective-permute-start | bytes 1769480 | tf_op jit(solution)/shard_map/ppermute | solution.py:507
  470.0 36.8 %collective-permute-start.75 = (bf16[1152,256]{1,0:T(8,128)(2,1)}, bf16[1152,256]{1,0:T(8,128)(2,1)S(1)}, u32[]{:S(2)}, u32[]{:S(2)}) collective-permute-start(bf16[1152,256]{1,0:T(8,128)(2,1)} %collective-permute-done.74.refs_0_), channel_id=1, source_target_pairs={{0,8},{8,16},{16,24},{24,28},{28,20},{20,12},{12,4},{4,0},{1,9},{9... | collective-permute-start | bytes 1769480 | tf_op jit(solution)/shard_map/ppermute | solution.py:507
  (146 other events, 2118.8 us)
